TPU v7x, 512 devices: a whole 4x8x8 slice. The times are simulated.
512 devices in a mesh: gs: 128 (over y, z, core), view: 4 (over x).
Axes of the slice: x: 4, y: 8, z: 8, core: 2. Of those that a mesh axis runs over, the one named last changes fastest.
Arguments:
- features: bfloat16 [131072, 128], P('gs'), may hold values from -6 to 6
- geometry: float32 [4, 9, 131072], P('view', None, 'gs'), as said below
- decoder: bfloat16 [128, 512], replicated, may hold values from -0.5 to 0.5
- teacher: bfloat16 [4, 131072, 512], P('view', 'gs'), may hold values from -3 to 3
- images: float32 [4, 3, 131072], P('view', None, 'gs'), may hold values from 0 to 1
- send_index: int32 [4, 128, 1024], P('view', 'gs'), may hold values from 0 to 1023, as said below
- tile_lists: int32 [4, 512, 8], P('view', 'gs'), may hold values from 0 to 7, as said below
- tile_lengths: int32 [4, 512], P('view', 'gs'), may hold values from 2 to 8
Outputs:
- feature_grad: float32 [131072, 128], P(('gs', 'view'))
- geometry_grad: float32 [4, 9, 131072], P('view', None, 'gs')
- decoder_grad: float32 [128, 512], replicated
Inputs may be any that keep to these rules, and one draw needn't show every extreme that they name: `send_index`: each row (one view, one source device) is a permutation of 0 .. 1023; positions k * 8 to (k + 1) * 8 - 1 hold the Gaussians sent to the device of gs index k. `tile_lists`: the 8 entries of a row are distinct. `geometry`: opacity logits lie in -7.5 .. -4, log conics between -2 log 16 and -2 log 16 + 2 log 4, shears in -2 .. 2, colors in 0 .. 1.
All inputs are finite; a program needn't handle non-finite values.
Results may differ from a plain program's by a relative error of at most 0.0017.
Values may be sent and summed in bfloat16 or wider, within the bound.
A program may use at most 64 MiB of HBM per device.

v0:
```python
import math

import jax
import jax.numpy as jnp
from jax import lax
from jax.sharding import PartitionSpec as P

FEAT = 128
CT = 512
TS = 16
BLK = 128
LIST = 8


def composite(tile_geo, alive_mask, pixel_x, pixel_y):
    delta_x = pixel_x[:, None] - tile_geo[0][None, :]
    delta_y = pixel_y[:, None] - tile_geo[1][None, :]
    conic_a = jnp.exp(tile_geo[2])
    conic_c = jnp.exp(tile_geo[3])
    conic_b = 0.8 * jnp.tanh(tile_geo[4]) * jnp.exp(0.5 * (tile_geo[2] + tile_geo[3]))
    exponent = -0.5 * (
        conic_a * delta_x * delta_x
        + 2.0 * conic_b * delta_x * delta_y
        + conic_c * delta_y * delta_y
    )
    opacity = alive_mask * jax.nn.sigmoid(tile_geo[5])
    alpha_val = opacity[None, :] * jnp.exp(exponent)
    log_keep = jnp.log1p(-alpha_val)
    pixel_count = pixel_x.shape[0]
    blocked = log_keep.reshape(pixel_count, LIST, BLK)
    inner = jnp.cumsum(blocked, axis=2) - blocked
    block_sums = jnp.sum(blocked, axis=2)
    outer = jnp.cumsum(block_sums, axis=1) - block_sums
    before = (inner + outer[:, :, None]).reshape(pixel_count, LIST * BLK)
    weights = alpha_val * jnp.exp(before)
    pixel_color = jnp.einsum("pi,ci->cp", weights, tile_geo[6:9], precision=lax.Precision.HIGHEST)
    return (weights, pixel_color)


def device_terms(
    recv_geo, recv_feat, decoder, teacher_dev, images_dev, lists, lengths, shard_index
):
    nblocks = recv_feat.shape[0] // BLK
    tile_pixels = TS * TS
    geo_blocks = recv_geo.reshape(9, nblocks, BLK)
    feat_blocks = recv_feat.reshape(nblocks, BLK, FEAT)
    within = jnp.arange(tile_pixels, dtype=jnp.int32)
    block_range = jnp.arange(nblocks, dtype=jnp.int32)
    slot_range = jnp.arange(LIST, dtype=jnp.int32)

    def tile_step(totals, tile_index):
        decoder_sum, geo_acc, feat_acc = totals
        block_ids = lists[tile_index]
        count = lengths[tile_index]
        alive_mask = jnp.broadcast_to(
            (slot_range < count).astype(jnp.float32)[:, None], (LIST, BLK)
        ).reshape(LIST * BLK)
        tile_geo = jnp.take(geo_blocks, block_ids, axis=1).reshape(9, LIST * BLK)
        feat_tile = jnp.take(feat_blocks, block_ids, axis=0).reshape(LIST * BLK, FEAT)
        column = 2 * TS * (shard_index % 30) + TS * (tile_index % 2) + within % TS
        row_index = 2 * TS * (shard_index // 30) + TS * (tile_index // 2) + within // TS
        pixel_x = column.astype(jnp.float32) + 0.5
        pixel_y = row_index.astype(jnp.float32) + 0.5
        (weights, pixel_color), pullback = jax.vjp(
            lambda geo_part: composite(geo_part, alive_mask, pixel_x, pixel_y), tile_geo
        )
        weight_b = weights.astype(jnp.bfloat16)
        rendered = jnp.dot(weight_b, feat_tile, preferred_element_type=jnp.float32).astype(
            jnp.bfloat16
        )
        pred = jnp.dot(rendered, decoder, preferred_element_type=jnp.float32)
        teacher_rows = lax.dynamic_slice_in_dim(
            teacher_dev, tile_index * tile_pixels, tile_pixels, 0
        )
        error_feat = pred - teacher_rows.astype(jnp.float32)
        gpred = (error_feat / jnp.sqrt(error_feat * error_feat + 0.04)).astype(jnp.bfloat16)
        grender = lax.dot_general(
            gpred, decoder, (((1,), (1,)), ((), ())), preferred_element_type=jnp.float32
        ).astype(jnp.bfloat16)
        decoder_sum = decoder_sum + lax.dot_general(
            rendered, gpred, (((0,), (0,)), ((), ())), preferred_element_type=jnp.float32
        )
        image_cols = lax.dynamic_slice_in_dim(images_dev, tile_index * tile_pixels, tile_pixels, 1)
        error_color = pixel_color - image_cols
        gcolor = error_color / jnp.sqrt(error_color * error_color + 0.04)
        gweight = lax.dot_general(
            grender, feat_tile, (((1,), (1,)), ((), ())), preferred_element_type=jnp.float32
        )
        gfeat_tile = lax.dot_general(
            weight_b, grender, (((0,), (0,)), ((), ())), preferred_element_type=jnp.float32
        )
        (ggeo_tile,) = pullback((gweight, gcolor))
        hits = (block_ids[:, None] == block_range[None, :]).astype(jnp.float32)
        geo_acc = geo_acc + jnp.einsum(
            "clb,ln->cnb", ggeo_tile.reshape(9, LIST, BLK), hits, precision=lax.Precision.HIGHEST
        )
        feat_acc = feat_acc + jnp.einsum(
            "ln,lbf->nbf",
            hits,
            gfeat_tile.reshape(LIST, BLK, FEAT),
            precision=lax.Precision.HIGHEST,
        )
        return ((decoder_sum, geo_acc, feat_acc), None)

    start_totals = (
        jnp.zeros((FEAT, CT), jnp.float32),
        jnp.zeros((9, nblocks, BLK), jnp.float32),
        jnp.zeros((nblocks, BLK, FEAT), jnp.float32),
    )
    tile_range = jnp.arange(lists.shape[0], dtype=jnp.int32)
    (decoder_sum, geo_acc, feat_acc), _ = lax.scan(tile_step, start_totals, tile_range)
    return (decoder_sum, geo_acc.reshape(9, nblocks * BLK), feat_acc.reshape(nblocks * BLK, FEAT))


def on_device(features, geometry, decoder, teacher, images, send_index, tile_lists, tile_lengths):
    send_order = send_index[0, 0]
    shard_index = lax.axis_index("gs")
    geo_send = jnp.take(geometry[0], send_order, axis=1)
    recv_geo = lax.all_to_all(geo_send, "gs", split_axis=1, concat_axis=1, tiled=True)
    feat_send = jnp.take(features, send_order, axis=0)
    recv_feat = lax.all_to_all(feat_send, "gs", split_axis=0, concat_axis=0, tiled=True)
    decoder_sum, geo_acc, feat_acc = device_terms(
        recv_geo,
        recv_feat,
        decoder,
        teacher[0],
        images[0],
        tile_lists[0],
        tile_lengths[0],
        shard_index,
    )
    returned_geo = lax.all_to_all(geo_acc, "gs", split_axis=1, concat_axis=1, tiled=True)
    returned_feat = lax.all_to_all(feat_acc, "gs", split_axis=0, concat_axis=0, tiled=True)
    geo_own = jnp.zeros_like(returned_geo).at[:, send_order].set(returned_geo)
    feat_own = jnp.zeros_like(returned_feat).at[send_order].set(returned_feat)
    quarter = feat_own.shape[0] // lax.axis_size("view")
    summed = lax.psum(feat_own, "view")
    feature_grad = lax.dynamic_slice_in_dim(summed, lax.axis_index("view") * quarter, quarter, 0)
    pixel_total = lax.axis_size("gs") * lax.axis_size("view") * tile_lists.shape[1] * TS * TS
    decoder_grad = lax.psum(decoder_sum, ("gs", "view")) * (1.0 / math.sqrt(pixel_total))
    return (feature_grad, geo_own[None], decoder_grad)


def solution(mesh):
    placed = (
        P("gs", None),
        P("view", None, "gs"),
        P(),
        P("view", "gs", None),
        P("view", None, "gs"),
        P("view", "gs", None),
        P("view", "gs", None),
        P("view", "gs"),
    )
    return jax.shard_map(
        on_device,
        mesh=mesh,
        in_specs=placed,
        out_specs=(P(("gs", "view"), None), P("view", None, "gs"), P()),
        check_vma=False,
    )
```

profile of v0, /device:TPU:1, one launch (start us, length us, event | category | flops | bytes accessed | tf_op | source)
XLA Modules:
  0.0 609.1 jit_solution(10011325874883574381)
XLA Ops:
  10.2 2.8 gather_fusion.2
  14.1 18.4 %all-to-all-start = ((f32[9,128,8]{0,2,1:T(8,128)}), f32[9,128,8]{0,2,1:T(8,128)S(1)}, u32[]{:S(2)}, u32[]{:S(2)}) async-start(f32[9,128,8]{0,2,1:T(8,128)} %bitcast_select_fusion.1), calls=%async_computation | async-start | bytes 1048576 | tf_op jit(solution)/shard_map/all_to_all | solution.py:119
  32.5 3.2 gather_fusion.3
  36.6 15.3 %all-to-all-done = f32[9,128,8]{0,2,1:T(8,128)S(1)} async-done(((f32[9,128,8]{0,2,1:T(8,128)}), f32[9,128,8]{0,2,1:T(8,128)S(1)}, u32[]{:S(2)}, u32[]{:S(2)}) %all-to-all-start) | async-done | bytes 36896 | tf_op jit(solution)/shard_map/all_to_all | solution.py:119
  52.0 7.2 %all-to-all-start.1 = ((bf16[128,8,128]{2,1,0:T(8,128)(2,1)}), bf16[128,8,128]{2,1,0:T(8,128)(2,1)S(1)}, u32[]{:S(2)}, u32[]{:S(2)}) async-start(bf16[128,8,128]{2,1,0:T(8,128)(2,1)} %bitcast_select_fusion.2), calls=%async_computation.1 | async-start | bytes 524288 | tf_op jit(solution)/shard_map/all_to_all | solution.py:121
  61.3 12.2 %all-to-all-done.1 = bf16[128,8,128]{2,1,0:T(8,128)(2,1)S(1)} async-done(((bf16[128,8,128]{2,1,0:T(8,128)(2,1)}), bf16[128,8,128]{2,1,0:T(8,128)(2,1)S(1)}, u32[]{:S(2)}, u32[]{:S(2)}) %all-to-all-start.1) | async-done | bytes 262176 | tf_op jit(solution)/shard_map/all_to_all | solution.py:121
  74.2 187.1 %while.21 = (s32[]{:T(128)}, f32[128,512]{1,0:T(8,128)}, f32[9,8,128]{2,1,0:T(8,128)}, f32[8,128,128]{2,0,1:T(8,128)}, s32[4]{0:T(128)S(1)}, /*index=5*/s32[4]{0...) while((s32[]{:T(128)}, f32[128,512]{1,0:T(8,128)}, ...), condition=%wide.region_13.14_spmd.clone.clone, body=%wide.region_0.13_spmd.clone.clone.sunk | while | flops 448201472 | bytes 62394652 | solution.py:111
  107.5 3.4 fusion.167
  115.2 2.3 fusion.168
  148.1 2.3 convolution_add_fusion.8
  154.6 3.4 fusion.167
  162.2 2.3 fusion.168
  201.6 3.4 fusion.167
  209.3 2.3 fusion.168
  248.6 3.4 fusion.167
  256.3 2.3 fusion.168
  263.2 6.9 %all-to-all-start.2 = ((f32[128,8,128]{2,1,0:T(8,128)}), f32[128,8,128]{2,1,0:T(8,128)S(1)}, u32[]{:S(2)}, u32[]{:S(2)}) async-start(f32[128,8,128]{2,1,0:T(8,128)} %bitcast.11), calls=%async_computation.2 | async-start | bytes 1048576 | tf_op jit(solution)/shard_map/all_to_all | solution.py:133
  270.9 18.8 %all-to-all-done.2 = f32[128,8,128]{2,1,0:T(8,128)S(1)} async-done(((f32[128,8,128]{2,1,0:T(8,128)}), f32[128,8,128]{2,1,0:T(8,128)S(1)}, u32[]{:S(2)}, u32[]{:S(2)}) %all-to-all-start.2) | async-done | bytes 524320 | tf_op jit(solution)/shard_map/all_to_all | solution.py:133
  289.7 4.0 scatter_custom_fusion
  295.6 7.1 %all-to-all-start.3 = ((f32[9,128,8]{0,2,1:T(8,128)}), f32[9,128,8]{0,2,1:T(8,128)S(1)}, u32[]{:S(2)}, u32[]{:S(2)}) async-start(f32[9,128,8]{0,2,1:T(8,128)} %bitcast.13), calls=%async_computation.3 | async-start | bytes 1048576 | tf_op jit(solution)/shard_map/all_to_all | solution.py:132
  302.7 19.7 %all-to-all-done.3 = f32[9,128,8]{0,2,1:T(8,128)S(1)} async-done(((f32[9,128,8]{0,2,1:T(8,128)}), f32[9,128,8]{0,2,1:T(8,128)S(1)}, u32[]{:S(2)}, u32[]{:S(2)}) %all-to-all-start.3) | async-done | bytes 36896 | tf_op jit(solution)/shard_map/all_to_all | solution.py:132
  322.4 3.4 scatter_custom_fusion.1
  326.6 223.9 %all-reduce.14.cloned.1.call-done = f32[128,512]{1,0:T(8,128)} async-done(((f32[128,512]{1,0:T(8,128)}), f32[128,512]{1,0:T(8,128)}) %all-reduce.14.cloned.1.call-update) | async-done | bytes 262160 | tf_op jit(solution)/shard_map/psum | solution.py:140
  552.1 48.6 %all-reduce.12.cloned.1.call-done = f32[1024,128]{1,0:T(8,128)} async-done(((f32[1024,128]{1,0:T(8,128)}), f32[1024,128]{1,0:T(8,128)}) %all-reduce.12.cloned.1.call-update) | async-done | bytes 524304 | tf_op jit(solution)/shard_map/psum | solution.py:137
  (525 shorter events, 158.1 us)
Async XLA Ops:
  7.2 25.3 %copy-start = (bf16[1024,128]{1,0:T(8,128)(2,1)S(1)}, bf16[1024,128]{1,0:T(8,128)(2,1)}, u32[]{:S(2)}) copy-start(bf16[1024,128]{1,0:T(8,128)(2,1)} %param.10) | copy-start | bytes 786436
  14.1 37.9 %all-to-all-start = ((f32[9,128,8]{0,2,1:T(8,128)}), f32[9,128,8]{0,2,1:T(8,128)S(1)}, u32[]{:S(2)}, u32[]{:S(2)}) async-start(f32[9,128,8]{0,2,1:T(8,128)} %bitcast_select_fusion.1), calls=%async_computation | async-start | bytes 1048576 | tf_op jit(solution)/shard_map/all_to_all | solution.py:119
  52.0 21.6 %all-to-all-start.1 = ((bf16[128,8,128]{2,1,0:T(8,128)(2,1)}), bf16[128,8,128]{2,1,0:T(8,128)(2,1)S(1)}, u32[]{:S(2)}, u32[]{:S(2)}) async-start(bf16[128,8,128]{2,1,0:T(8,128)(2,1)} %bitcast_select_fusion.2), calls=%async_computation.1 | async-start | bytes 524288 | tf_op jit(solution)/shard_map/all_to_all | solution.py:121
  81.8 22.9 %copy-start.21 = (f32[256]{0:T(256)}, f32[256]{0:T(256)S(1)}, u32[]{:S(2)}) copy-start(f32[256]{0:T(256)S(1)} %get-tuple-element.768) | copy-start | bytes 3076 | tf_op jit(solution)/shard_map/while
  81.8 22.9 %copy-start.23 = (f32[256]{0:T(256)}, f32[256]{0:T(256)S(1)}, u32[]{:S(2)}) copy-start(f32[256]{0:T(256)S(1)} %get-tuple-element.765) | copy-start | bytes 3076 | tf_op jit(solution)/shard_map/while
  127.8 24.0 %copy-start.21 = (f32[256]{0:T(256)}, f32[256]{0:T(256)S(1)}, u32[]{:S(2)}) copy-start(f32[256]{0:T(256)S(1)} %get-tuple-element.768) | copy-start | bytes 3076 | tf_op jit(solution)/shard_map/while
  127.8 24.0 %copy-start.23 = (f32[256]{0:T(256)}, f32[256]{0:T(256)S(1)}, u32[]{:S(2)}) copy-start(f32[256]{0:T(256)S(1)} %get-tuple-element.765) | copy-start | bytes 3076 | tf_op jit(solution)/shard_map/while
  130.7 20.0 %copy-start.5 = (f32[9,8,128]{2,0,1:T(8,128)}, f32[9,8,128]{2,0,1:T(8,128)S(1)}, u32[]{:S(2)}) copy-start(f32[9,8,128]{2,0,1:T(8,128)S(1)} %select_bitcast_fusion.2) | copy-start | bytes 110596 | tf_op jit(solution)/shard_map/while
  131.3 20.5 %copy-start.11 = (f32[1,8,128]{2,0,1:T(1,128)}, f32[1,8,128]{2,0,1:T(1,128)S(1)}, u32[]{:S(2)}) copy-start(f32[1,8,128]{2,0,1:T(1,128)S(1)} %get-tuple-element.769) | copy-start | bytes 12292 | tf_op jit(solution)/shard_map/while
  131.9 19.9 %copy-start.16 = (f32[1024]{0:T(1024)}, f32[1024]{0:T(1024)S(1)}, u32[]{:S(2)}) copy-start(f32[1024]{0:T(1024)S(1)} %bitcast_multiply_fusion.8) | copy-start | bytes 12292 | tf_op jit(solution)/shard_map/while
  174.8 24.0 %copy-start.21 = (f32[256]{0:T(256)}, f32[256]{0:T(256)S(1)}, u32[]{:S(2)}) copy-start(f32[256]{0:T(256)S(1)} %get-tuple-element.768) | copy-start | bytes 3076 | tf_op jit(solution)/shard_map/while
  174.8 24.0 %copy-start.23 = (f32[256]{0:T(256)}, f32[256]{0:T(256)S(1)}, u32[]{:S(2)}) copy-start(f32[256]{0:T(256)S(1)} %get-tuple-element.765) | copy-start | bytes 3076 | tf_op jit(solution)/shard_map/while
  177.7 20.0 %copy-start.5 = (f32[9,8,128]{2,0,1:T(8,128)}, f32[9,8,128]{2,0,1:T(8,128)S(1)}, u32[]{:S(2)}) copy-start(f32[9,8,128]{2,0,1:T(8,128)S(1)} %select_bitcast_fusion.2) | copy-start | bytes 110596 | tf_op jit(solution)/shard_map/while
  178.4 20.5 %copy-start.11 = (f32[1,8,128]{2,0,1:T(1,128)}, f32[1,8,128]{2,0,1:T(1,128)S(1)}, u32[]{:S(2)}) copy-start(f32[1,8,128]{2,0,1:T(1,128)S(1)} %get-tuple-element.769) | copy-start | bytes 12292 | tf_op jit(solution)/shard_map/while
  178.9 19.9 %copy-start.16 = (f32[1024]{0:T(1024)}, f32[1024]{0:T(1024)S(1)}, u32[]{:S(2)}) copy-start(f32[1024]{0:T(1024)S(1)} %bitcast_multiply_fusion.8) | copy-start | bytes 12292 | tf_op jit(solution)/shard_map/while
  221.8 24.0 %copy-start.21 = (f32[256]{0:T(256)}, f32[256]{0:T(256)S(1)}, u32[]{:S(2)}) copy-start(f32[256]{0:T(256)S(1)} %get-tuple-element.768) | copy-start | bytes 3076 | tf_op jit(solution)/shard_map/while
  221.8 24.0 %copy-start.23 = (f32[256]{0:T(256)}, f32[256]{0:T(256)S(1)}, u32[]{:S(2)}) copy-start(f32[256]{0:T(256)S(1)} %get-tuple-element.765) | copy-start | bytes 3076 | tf_op jit(solution)/shard_map/while
  224.8 20.0 %copy-start.5 = (f32[9,8,128]{2,0,1:T(8,128)}, f32[9,8,128]{2,0,1:T(8,128)S(1)}, u32[]{:S(2)}) copy-start(f32[9,8,128]{2,0,1:T(8,128)S(1)} %select_bitcast_fusion.2) | copy-start | bytes 110596 | tf_op jit(solution)/shard_map/while
  225.4 20.5 %copy-start.11 = (f32[1,8,128]{2,0,1:T(1,128)}, f32[1,8,128]{2,0,1:T(1,128)S(1)}, u32[]{:S(2)}) copy-start(f32[1,8,128]{2,0,1:T(1,128)S(1)} %get-tuple-element.769) | copy-start | bytes 12292 | tf_op jit(solution)/shard_map/while
  226.0 19.9 %copy-start.16 = (f32[1024]{0:T(1024)}, f32[1024]{0:T(1024)S(1)}, u32[]{:S(2)}) copy-start(f32[1024]{0:T(1024)S(1)} %bitcast_multiply_fusion.8) | copy-start | bytes 12292 | tf_op jit(solution)/shard_map/while
  263.2 26.5 %all-to-all-start.2 = ((f32[128,8,128]{2,1,0:T(8,128)}), f32[128,8,128]{2,1,0:T(8,128)S(1)}, u32[]{:S(2)}, u32[]{:S(2)}) async-start(f32[128,8,128]{2,1,0:T(8,128)} %bitcast.11), calls=%async_computation.2 | async-start | bytes 1048576 | tf_op jit(solution)/shard_map/all_to_all | solution.py:133
  270.2 280.3 %all-reduce.14.cloned.1.call-start = ((), (), s32[]{:S(2)}) async-start(), calls=%async_computation.5 | async-start | bytes 524288 | tf_op jit(solution)/shard_map/psum | solution.py:140
  270.9 329.8 %all-reduce.12.cloned.1.call-start = ((), (), s32[]{:S(2)}) async-start(), calls=%async_computation.4 | async-start | bytes 1048576 | tf_op jit(solution)/shard_map/psum | solution.py:137
  295.6 26.8 %all-to-all-start.3 = ((f32[9,128,8]{0,2,1:T(8,128)}), f32[9,128,8]{0,2,1:T(8,128)S(1)}, u32[]{:S(2)}, u32[]{:S(2)}) async-start(f32[9,128,8]{0,2,1:T(8,128)} %bitcast.13), calls=%async_computation.3 | async-start | bytes 1048576 | tf_op jit(solution)/shard_map/all_to_all | solution.py:132
  (113 other events, 331.2 us)
Sparse Core Ops, SparseCore 0:
  276.6 273.8 all-reduce.13
  552.9 47.7 all-reduce.11
where the time goes:
time: 613 us; the launch traced here: 609 us
  waiting for transfers between devices  339 us (55%)
  local copies, waits for them, and re-layouts  79.9 us (13%)
  other arithmetic  76.6 us (12%)
  starting transfers between devices  39.8 us (6%)
  matrix products  39.1 us (6%)
  loops' own time  20.3 us (3%)
  between operations  14.3 us (2%)
    psum x1, waiting for transfers between devices, on_device(): lax.psum(decoder_sum, ('gs', 'view')) * (1.0 / math.sqrt(pixel_total))  224 us
    psum x1, waiting for transfers between devices, on_device(): summed = lax.psum(feat_own, 'view')  48.6 us
    another operation x8, other arithmetic, composite(): inner = jnp.cumsum(blocked, axis=2) - blocked  22.4 us
    another operation x1, loops' own time, device_terms(): lax.scan(tile_step, start_totals, tile_range)  20.3 us
    all_to_all x1, waiting for transfers between devices, on_device(): lax.all_to_all(geo_acc, 'gs', split_axis=1, concat_axis=1, tiled=True)  19.7 us
    while x264, local copies, waits for them, and re-layouts  19.3 us
    all_to_all x1, waiting for transfers between devices, on_device(): lax.all_to_all(feat_acc, 'gs', split_axis=0, concat_axis=0, tiled=True)  18.8 us
    all_to_all x1, starting transfers between devices, on_device(): lax.all_to_all(geo_send, 'gs', split_axis=1, concat_axis=1, tiled=True)  18.4 us
  transfers between devices with their start and end apart: 6, of which 6 were waited for; matrix products, arithmetic and copies ran while one was open for 3% of the time, Pallas kernels for 0%

commit v1 on v0

v1 whole, which is shorter than its diff:
```python
import functools, math
import numpy as np
import jax, jax.numpy as jnp
from jax import lax
from jax.experimental import pallas as pl
from jax.experimental.pallas import tpu as pltpu
from jax.sharding import PartitionSpec as P

FEAT = 128
CT = 512
TS = 16
BLK = 128
LIST = 8
PIX = TS * TS
F32 = jnp.float32
BF16 = jnp.bfloat16
LOG2E = 1.4426950408889634


def pixel_tables(tiles):
    q = np.arange(PIX)
    basis = np.zeros((tiles, 128, PIX), np.float32)
    moments = np.zeros((tiles, PIX, 128), np.float32)
    for k in range(tiles):
        px = TS * (k % 2) + q % TS + 0.5 - TS
        py = TS * (k // 2) + q // TS + 0.5 - TS
        rows = [np.ones(PIX), px, py]
        for square in (px * px, px * py, py * py):
            high = square.astype(jnp.bfloat16).astype(np.float64)
            rows += [high, square - high]
        row = 32
        for index, values in enumerate(rows):
            basis[k, row : row + 3] = values
            row += 3
            moments[k, :, 32 + index] = values
    return basis.astype(jnp.bfloat16), moments.astype(jnp.bfloat16)


def order_tables():
    i = np.arange(BLK)
    before = (i[None, :] < i[:, None]).astype(np.float32)
    after = (i[None, :] > i[:, None]).astype(np.float32)
    return np.stack(
        [np.concatenate([before, before], 1), np.concatenate([after, after], 1)]
    ).astype(jnp.bfloat16)


def pieces(x, count):
    parts = []
    for _ in range(count):
        part = x.astype(BF16)
        parts.append(part)
        x = x - part.astype(F32)
    return parts


def dot(a, b):
    return jnp.dot(a, b, preferred_element_type=F32)


def tiles_kernel(
    lists_ref, lengths_ref, base_ref,
    geo_ref, feat_ref, decoder_ref, teacher_ref, images_ref, basis_ref, moments_ref, order_ref,
    geo_grad_ref, feat_grad_ref, decoder_grad_ref,
    rows, columns, feat_t, alphas, weights, weights_b, terms, right, small,
):
    tile = pl.program_id(0)
    tiles = pl.num_programs(0)
    count = geo_ref.shape[1]
    nblocks = count // BLK

    def parameters():
        x = jnp.clip(geo_ref[0:1, :] - base_ref[0], -4096.0, 4096.0)
        y = jnp.clip(geo_ref[1:2, :] - base_ref[1], -4096.0, 4096.0)
        a = jnp.exp(geo_ref[2:3, :])
        c = jnp.exp(geo_ref[3:4, :])
        slope = jnp.tanh(geo_ref[4:5, :])
        scale = 0.8 * jnp.exp(0.5 * (geo_ref[2:3, :] + geo_ref[3:4, :]))
        return x, y, a, c, slope, scale

    @pl.when(tile == 0)
    def _():
        rows[...] = jnp.zeros_like(rows)
        feat_grad_ref[...] = jnp.zeros_like(feat_grad_ref)
        decoder_grad_ref[...] = jnp.zeros_like(decoder_grad_ref)
        small[...] = jnp.zeros_like(small)
        x, y, a, c, slope, scale = parameters()
        b = slope * scale
        logit = geo_ref[5:6, :]
        log_opacity = -jnp.log(1.0 + jnp.exp(-logit))
        ax_by = a * x + b * y
        bx_cy = b * x + c * y
        constant = log_opacity - 0.5 * (x * ax_by + y * bx_cy)
        row = 32
        for coefficient, repeats in (
            (constant, 1), (ax_by, 1), (bx_cy, 1), (-0.5 * a, 2), (-b, 2), (-0.5 * c, 2)
        ):
            parts = pieces(coefficient * LOG2E, 3)
            for _ in range(repeats):
                for part in parts:
                    rows[row : row + 1, :] = part.astype(F32)
                    row += 1
        high, middle, low = pieces(geo_ref[6:9, :], 3)
        for index, part in enumerate((high, high, middle, high, middle, low)):
            rows[3 * index : 3 * index + 3, :] = part.astype(F32)
        for n in range(nblocks):
            span = slice(n * BLK, (n + 1) * BLK)
            columns[span, 0:BLK] = feat_ref[span, :]
            columns[span, BLK : 2 * BLK] = rows[:, span].T.astype(BF16)
            feat_t[n, 0:FEAT, :] = feat_ref[span, :].astype(F32).T.astype(BF16)
            feat_t[n, FEAT : FEAT + 32, :] = rows[0:32, span].astype(BF16)

    length = lengths_ref[tile]
    ids = [lists_ref[tile, slot] for slot in range(LIST)]
    starts = [pl.multiple_of(block * BLK, BLK) for block in ids]
    before = order_ref[0]
    after = order_ref[1]
    basis = basis_ref[0]

    carry = jnp.zeros((1, PIX), F32)
    acc = jnp.zeros((FEAT + 32, PIX), F32)
    acc_low = jnp.zeros((32, PIX), F32)
    for slot in range(LIST):
        span = slice(slot * BLK, (slot + 1) * BLK)
        exponent = dot(columns[pl.ds(starts[slot], BLK), BLK : 2 * BLK], basis)
        exponent = jnp.where(slot < length, exponent, -1e30)
        alpha = jnp.exp2(exponent)
        log_keep = alpha * (-LOG2E + alpha * (-LOG2E / 2 + alpha * (-LOG2E / 3 + alpha * (-LOG2E / 4))))
        high, low = pieces(log_keep, 2)
        inner = dot(before, jnp.concatenate([high, low], 0))
        weight = alpha * jnp.exp2(inner + carry)
        carry = carry + inner[BLK - 1 : BLK, :] + log_keep[BLK - 1 : BLK, :]
        weight_b, weight_low = pieces(weight, 2)
        alphas[span, :] = alpha
        weights[span, :] = weight
        weights_b[span, 0:PIX] = weight_b
        weights_b[span, PIX : 2 * PIX] = weight_low
        acc = acc + dot(feat_t[ids[slot]], weight_b)
        acc_low = acc_low + dot(feat_t[ids[slot], FEAT : FEAT + 32, :], weight_low)

    rendered_t = acc[0:FEAT, :].astype(BF16)
    color = (
        acc[FEAT : FEAT + 3] + acc[FEAT + 6 : FEAT + 9] + acc[FEAT + 15 : FEAT + 18]
        + acc_low[0:3] + acc_low[6:9]
    )
    error_color = color - images_ref[...]
    gcolor = error_color * lax.rsqrt(error_color * error_color + 0.04)
    rendered = acc[0:FEAT, :].T.astype(BF16)
    pred = dot(rendered, decoder_ref[...])
    error = pred - teacher_ref[...].astype(F32)
    gpred = (error * lax.rsqrt(error * error + 0.04)).astype(BF16)
    decoder_grad_ref[...] += dot(rendered_t, gpred)
    grender_t = lax.dot_general(
        decoder_ref[...], gpred, (((1,), (1,)), ((), ())), preferred_element_type=F32
    )
    terms[0:FEAT, :] = grender_t
    terms[FEAT:, :] = jnp.zeros_like(terms[FEAT:, :])
    high, middle, low = pieces(gcolor, 3)
    for index, part in enumerate((high, middle, high, low, middle, high)):
        terms[FEAT + 3 * index : FEAT + 3 * index + 3, :] = part.astype(F32)
    left = terms[...].astype(BF16)
    right[...] = terms[...].T.astype(BF16)
    moments = moments_ref[0]

    carry = jnp.zeros((1, PIX), F32)
    for slot in reversed(range(LIST)):
        span = slice(slot * BLK, (slot + 1) * BLK)
        gweight = dot(columns[pl.ds(starts[slot], BLK), :], left)
        value = gweight * weights[span, :]
        high, low = pieces(value, 2)
        inner = dot(after, jnp.concatenate([high, low], 0))
        alpha = alphas[span, :]
        square = alpha * alpha
        ratio = alpha + square
        ratio = ratio + ratio * square
        ratio = ratio + ratio * (square * square)
        gexponent = value - ratio * (inner + carry)
        carry = carry + inner[0:1, :] + value[0:1, :]
        high, low = pieces(gexponent, 2)
        wide = dot(weights_b[span, 0:PIX], right[...])
        narrow = dot(weights_b[span, PIX : 2 * PIX], right[:, FEAT : 2 * FEAT])
        narrow = narrow + dot(high, moments) + dot(low, moments)
        where = pl.ds(starts[slot], BLK)
        feat_grad_ref[where, :] += wide[:, 0:FEAT]
        small[where, :] += wide[:, FEAT : 2 * FEAT] + narrow

    @pl.when(tile == tiles - 1)
    def _():
        for n in range(nblocks):
            span = slice(n * BLK, (n + 1) * BLK)
            rows[:, span] = small[span, :].T
        x, y, a, c, slope, scale = parameters()
        b = slope * scale
        s0, sx, sy = (rows[32 + i : 33 + i, :] for i in range(3))
        sxx, sxy, syy = (rows[35 + 2 * i : 36 + 2 * i, :] + rows[36 + 2 * i : 37 + 2 * i, :] for i in range(3))
        ux = sx - x * s0
        uy = sy - y * s0
        dxx = sxx - 2.0 * x * sx + x * x * s0
        dyy = syy - 2.0 * y * sy + y * y * s0
        dxy = sxy - x * sy - y * sx + x * y * s0
        geo_grad_ref[0:1, :] = a * ux + b * uy
        geo_grad_ref[1:2, :] = b * ux + c * uy
        geo_grad_ref[2:3, :] = -0.5 * (a * dxx + b * dxy)
        geo_grad_ref[3:4, :] = -0.5 * (c * dyy + b * dxy)
        geo_grad_ref[4:5, :] = -dxy * scale * (1.0 - slope * slope)
        geo_grad_ref[5:6, :] = s0 / (1.0 + jnp.exp(geo_ref[5:6, :]))
        geo_grad_ref[6:9, :] = rows[0:3, :] + rows[3:6, :] + rows[9:12, :]


def device_terms(recv_geo, recv_feat, decoder, teacher, images, lists, lengths, shard_index):
    tiles = lists.shape[0]
    count = recv_feat.shape[0]
    basis, moments = pixel_tables(tiles)
    base = jnp.stack([2 * TS * (shard_index % 30) + TS, 2 * TS * (shard_index // 30) + TS]).astype(F32)
    smem = pl.BlockSpec(memory_space=pltpu.SMEM)

    def whole(shape):
        return pl.BlockSpec(shape, lambda k: (0,) * len(shape))

    geo, feat, dec = pl.pallas_call(
        tiles_kernel,
        grid=(tiles,),
        in_specs=[
            smem, smem, smem,
            whole((9, count)), whole((count, FEAT)), whole((FEAT, CT)),
            pl.BlockSpec((PIX, CT), lambda k: (k, 0)),
            pl.BlockSpec((3, PIX), lambda k: (0, k)),
            pl.BlockSpec((1, 128, PIX), lambda k: (k, 0, 0)),
            pl.BlockSpec((1, PIX, 128), lambda k: (k, 0, 0)),
            whole((2, BLK, 2 * BLK)),
        ],
        out_specs=[whole((9, count)), whole((count, FEAT)), whole((FEAT, CT))],
        out_shape=[
            jax.ShapeDtypeStruct((9, count), F32),
            jax.ShapeDtypeStruct((count, FEAT), F32),
            jax.ShapeDtypeStruct((FEAT, CT), F32),
        ],
        scratch_shapes=[
            pltpu.VMEM((128, count), F32),
            pltpu.VMEM((count, 2 * BLK), BF16),
            pltpu.VMEM((count // BLK, FEAT + 32, BLK), BF16),
            pltpu.VMEM((LIST * BLK, PIX), F32),
            pltpu.VMEM((LIST * BLK, PIX), F32),
            pltpu.VMEM((LIST * BLK, 2 * PIX), BF16),
            pltpu.VMEM((2 * FEAT, PIX), F32),
            pltpu.VMEM((PIX, 2 * FEAT), BF16),
            pltpu.VMEM((count, 128), F32),
        ],
        compiler_params=pltpu.CompilerParams(dimension_semantics=("arbitrary",)),
        name="tiles",
    )(lists, lengths, base, recv_geo, recv_feat, decoder, teacher, images,
      jnp.asarray(basis), jnp.asarray(moments), jnp.asarray(order_tables()))
    return dec, geo, feat


def on_device(features, geometry, decoder, teacher, images, send_index, tile_lists, tile_lengths):
    send_order = send_index[0, 0]
    shard_index = lax.axis_index("gs")
    geo_send = jnp.take(geometry[0], send_order, axis=1)
    recv_geo = lax.all_to_all(geo_send, "gs", split_axis=1, concat_axis=1, tiled=True)
    feat_send = jnp.take(features, send_order, axis=0)
    recv_feat = lax.all_to_all(feat_send, "gs", split_axis=0, concat_axis=0, tiled=True)
    decoder_sum, geo_acc, feat_acc = device_terms(
        recv_geo, recv_feat, decoder, teacher[0], images[0], tile_lists[0], tile_lengths[0], shard_index
    )
    returned_geo = lax.all_to_all(geo_acc, "gs", split_axis=1, concat_axis=1, tiled=True)
    returned_feat = lax.all_to_all(feat_acc, "gs", split_axis=0, concat_axis=0, tiled=True)
    geo_own = jnp.zeros_like(returned_geo).at[:, send_order].set(returned_geo)
    feat_own = jnp.zeros_like(returned_feat).at[send_order].set(returned_feat)
    feature_grad = lax.psum_scatter(feat_own, "view", scatter_dimension=0, tiled=True)
    pixel_total = lax.axis_size("gs") * lax.axis_size("view") * tile_lists.shape[1] * PIX
    decoder_grad = lax.psum(decoder_sum, ("gs", "view")) * (1.0 / math.sqrt(pixel_total))
    return (feature_grad, geo_own[None], decoder_grad)


def solution(mesh):
    placed = (
        P("gs", None),
        P("view", None, "gs"),
        P(),
        P("view", "gs", None),
        P("view", None, "gs"),
        P("view", "gs", None),
        P("view", "gs", None),
        P("view", "gs"),
    )
    return jax.shard_map(
        on_device,
        mesh=mesh,
        in_specs=placed,
        out_specs=(P(("gs", "view"), None), P("view", None, "gs"), P()),
        check_vma=False,
    )
```

time: 613 us -> 396 us (0.65)
  other arithmetic: 76.6 us -> 5.68 us
  waiting for transfers between devices: 339 us -> 271 us
  local copies, waits for them, and re-layouts: 79.9 us -> 19.4 us
  matrix products: 39.1 us -> 0 us
  blocking collectives: 0 us -> 26.2 us
  Pallas kernels: 0 us -> 24 us
  loops' own time: 20.3 us -> 0 us
  starting transfers between devices: 39.8 us -> 32.8 us
    psum x1 -> x0, waiting for transfers between devices: 48.6 us -> none  [on_device(): summed = lax.psum(feat_own, 'view')]
    dot_general x44 -> x0, matrix products: 39.1 us -> none  [the longest x12 17.3 us: composite(): jnp.einsum('pi,ci->cp', weights, tile_geo[6:9], precision=lax.Precision.H...]
    all_to_all x0 -> x1, blocking collectives: none -> 26.2 us  [on_device(): lax.all_to_all(geo_acc, 'gs', split_axis=1, concat_axis=1, tiled=True)]
    another operation x16 -> x0, other arithmetic: 25.9 us -> none  [the longest x8 22.4 us: composite(): inner = jnp.cumsum(blocked, axis=2) - blocked]
    pallas_call x0 -> x1, Pallas kernels: none -> 24 us  [device_terms(): pl.pallas_call(tiles_kernel, grid=(tiles,), in_specs=[smem, smem, smem, w...]
    while x265 -> x0, local copies, waits for them, and re-layouts: 21.2 us -> none
    another operation x1 -> x0, loops' own time: 20.3 us -> none  [device_terms(): lax.scan(tile_step, start_totals, tile_range)]
    all_to_all x1 -> x0, waiting for transfers between devices: 19.7 us -> none  [on_device(): lax.all_to_all(geo_acc, 'gs', split_axis=1, concat_axis=1, tiled=True)]
  transfers between devices with their start and end apart: 6 -> 5, of which waited for: 6 -> 4; matrix products, arithmetic and copies ran while one was open for 3% -> 4% of each run, Pallas kernels for 0% -> 0%
where the time goes in v1:
time: 396 us; the launch traced here: 395 us
  waiting for transfers between devices  271 us (68%)
  starting transfers between devices  32.8 us (8%)
  blocking collectives  26.2 us (7%)
  Pallas kernels  24 us (6%)
  local copies, waits for them, and re-layouts  19.4 us (5%)
  between operations  15.6 us (4%)
  other arithmetic  5.68 us (1%)
    psum x1, waiting for transfers between devices, on_device(): lax.psum(decoder_sum, ('gs', 'view')) * (1.0 / math.sqrt(pixel_total))  225 us
    all_to_all x1, blocking collectives, on_device(): lax.all_to_all(geo_acc, 'gs', split_axis=1, concat_axis=1, tiled=True)  26.2 us
    pallas_call x1, Pallas kernels, device_terms(): pl.pallas_call(tiles_kernel, grid=(tiles,), in_specs=[smem, smem, smem, w...  24 us
    all_to_all x1, waiting for transfers between devices, on_device(): lax.all_to_all(feat_acc, 'gs', split_axis=0, concat_axis=0, tiled=True)  18.6 us
    all_to_all x1, starting transfers between devices, on_device(): lax.all_to_all(geo_send, 'gs', split_axis=1, concat_axis=1, tiled=True)  18.4 us
    all_to_all x1, waiting for transfers between devices, on_device(): lax.all_to_all(geo_send, 'gs', split_axis=1, concat_axis=1, tiled=True)  15.3 us
    all_to_all x1, waiting for transfers between devices, on_device(): lax.all_to_all(feat_send, 'gs', split_axis=0, concat_axis=0, tiled=True)  11.5 us
  transfers between devices with their start and end apart: 5, of which 4 were waited for; matrix products, arithmetic and copies ran while one was open for 4% of the time, Pallas kernels for 0%

profile of v1, /device:TPU:1, one launch (start us, length us, event | category | flops | bytes accessed | tf_op | source)
XLA Modules:
  0.0 394.9 jit_solution(14020480527548558939)
XLA Ops:
  8.0 0.8 compare_select_fusion.1
  10.1 0.7 copy-done.3
  11.1 2.8 gather_fusion
  13.9 1.0 bitcast_select_fusion
  14.9 18.4 %all-to-all-start = ((f32[9,128,8]{0,2,1:T(8,128)}), f32[9,128,8]{0,2,1:T(8,128)S(1)}, u32[]{:S(2)}, u32[]{:S(2)}) async-start(f32[9,128,8]{0,2,1:T(8,128)} %bitcast_select_fusion), calls=%async_computation | async-start | bytes 1048576 | tf_op jit(solution)/shard_map/all_to_all | solution.py:260
  33.3 3.2 gather_fusion.1
  36.5 0.9 bitcast_select_fusion.1
  37.4 15.3 %all-to-all-done = f32[9,128,8]{0,2,1:T(8,128)S(1)} async-done(((f32[9,128,8]{0,2,1:T(8,128)}), f32[9,128,8]{0,2,1:T(8,128)S(1)}, u32[]{:S(2)}, u32[]{:S(2)}) %all-to-all-start) | async-done | bytes 36896 | tf_op jit(solution)/shard_map/all_to_all | solution.py:260
  52.8 7.2 %all-to-all-start.1 = ((bf16[128,8,128]{2,1,0:T(8,128)(2,1)}), bf16[128,8,128]{2,1,0:T(8,128)(2,1)S(1)}, u32[]{:S(2)}, u32[]{:S(2)}) async-start(bf16[128,8,128]{2,1,0:T(8,128)(2,1)} %bitcast_select_fusion.1), calls=%async_computation.1 | async-start | bytes 524288 | tf_op jit(solution)/shard_map/all_to_all | solution.py:262
  60.1 0.7 copy-done.5
  62.0 0.8 copy.32.geo_ref
  62.8 11.5 %all-to-all-done.1 = bf16[128,8,128]{2,1,0:T(8,128)(2,1)S(1)} async-done(((bf16[128,8,128]{2,1,0:T(8,128)(2,1)}), bf16[128,8,128]{2,1,0:T(8,128)(2,1)S(1)}, u32[]{:S(2)}, u32[]{:S(2)}) %all-to-all-start.1) | async-done | bytes 262176 | tf_op jit(solution)/shard_map/all_to_all | solution.py:262
  74.4 0.7 copy-done.1
  75.1 24.0 %tiles.1 = (f32[9,1024]{1,0:T(8,128)}, f32[1024,128]{1,0:T(8,128)}, f32[128,512]{1,0:T(8,128)}) custom-call(s32[4,8]{1,0:T(4,128)} %bitcast.45, s32[4]{0:T(128)} %bitcast.46, f32[2]{0:T(128)} %add_convert_fusion.base_ref, f32[9,1024]{1,0:T(8,128)} %copy.32.geo_ref, bf16[1024,128]{1,0:T(8,128)(2,1)} %bitcast.38, bf16[128,512]{1,0:T(8,128)(2,1)} %decoder_ref.1, ...), custom_call_target="tpu_custom_call" | custom-call | tf_op jit(solution)/shard_map/tiles/pallas_call | solution.py:220
  99.1 6.9 %all-to-all-start.2 = ((f32[128,8,128]{2,1,0:T(8,128)}), f32[128,8,128]{2,1,0:T(8,128)S(1)}, u32[]{:S(2)}, u32[]{:S(2)}) async-start(f32[128,8,128]{2,1,0:T(8,128)} %bitcast.40), calls=%async_computation.2 | async-start | bytes 1048576 | tf_op jit(solution)/shard_map/all_to_all | solution.py:267
  106.1 0.7 all-reduce.2.cloned.1.call-update
  107.0 18.6 %all-to-all-done.2 = f32[128,8,128]{2,1,0:T(8,128)S(1)} async-done(((f32[128,8,128]{2,1,0:T(8,128)}), f32[128,8,128]{2,1,0:T(8,128)S(1)}, u32[]{:S(2)}, u32[]{:S(2)}) %all-to-all-start.2) | async-done | bytes 524320 | tf_op jit(solution)/shard_map/all_to_all | solution.py:267
  125.6 3.9 scatter_custom_fusion
  129.5 0.8 copy-done.2
  130.6 26.2 %all_to_all.40 = f32[9,128,8]{0,2,1:T(8,128)S(1)} all-to-all(f32[9,128,8]{0,2,1:T(8,128)S(1)} %bitcast.36), channel_id=1, replica_groups=mesh['gs'=128,'view'=4] {'gs'}, dimensions={1} | all-to-all | bytes 73728 | tf_op jit(solution)/shard_map/all_to_all | solution.py:266
  156.7 3.2 scatter_custom_fusion.1
  160.0 0.8 copy.31
  160.8 225.0 %all-reduce.2.cloned.1.call-done = f32[128,512]{1,0:T(8,128)} async-done(((f32[128,512]{1,0:T(8,128)}), f32[128,512]{1,0:T(8,128)}) %all-reduce.2.cloned.1.call-update) | async-done | bytes 262160 | tf_op jit(solution)/shard_map/psum | solution.py:272
  385.8 1.7 broadcast_multiply_fusion
  (21 shorter events, 3.3 us)
Async XLA Ops:
  8.0 25.3 %copy-start = (bf16[1024,128]{1,0:T(8,128)(2,1)S(1)}, bf16[1024,128]{1,0:T(8,128)(2,1)}, u32[]{:S(2)}) copy-start(bf16[1024,128]{1,0:T(8,128)(2,1)} %param.11) | copy-start | bytes 786436
  8.0 1.3 copy-start.4
  10.1 0.8 copy-start.3
  14.9 37.9 %all-to-all-start = ((f32[9,128,8]{0,2,1:T(8,128)}), f32[9,128,8]{0,2,1:T(8,128)S(1)}, u32[]{:S(2)}, u32[]{:S(2)}) async-start(f32[9,128,8]{0,2,1:T(8,128)} %bitcast_select_fusion), calls=%async_computation | async-start | bytes 1048576 | tf_op jit(solution)/shard_map/all_to_all | solution.py:260
  52.8 21.6 %all-to-all-start.1 = ((bf16[128,8,128]{2,1,0:T(8,128)(2,1)}), bf16[128,8,128]{2,1,0:T(8,128)(2,1)S(1)}, u32[]{:S(2)}, u32[]{:S(2)}) async-start(bf16[128,8,128]{2,1,0:T(8,128)(2,1)} %bitcast_select_fusion.1), calls=%async_computation.1 | async-start | bytes 524288 | tf_op jit(solution)/shard_map/all_to_all | solution.py:262
  60.0 0.7 copy-start.5
  74.4 0.7 copy-start.1
  99.1 26.5 %all-to-all-start.2 = ((f32[128,8,128]{2,1,0:T(8,128)}), f32[128,8,128]{2,1,0:T(8,128)S(1)}, u32[]{:S(2)}, u32[]{:S(2)}) async-start(f32[128,8,128]{2,1,0:T(8,128)} %bitcast.40), calls=%async_computation.2 | async-start | bytes 1048576 | tf_op jit(solution)/shard_map/all_to_all | solution.py:267
  106.0 279.8 %all-reduce.2.cloned.1.call-start = ((), (), s32[]{:S(2)}) async-start(), calls=%async_computation.6 | async-start | bytes 524288 | tf_op jit(solution)/shard_map/psum | solution.py:272
  106.8 280.7 %reduce-scatter.2.cloned.1.call-start = ((), (), s32[]{:S(2)}) async-start(), calls=%async_computation.5 | async-start | bytes 655360 | tf_op jit(solution)/shard_map/reduce_scatter | solution.py:270
  129.5 0.8 copy-start.2
Sparse Core Ops, SparseCore 0:
  111.8 273.9 all-reduce.1
Sparse Core Ops, SparseCore 1:
  129.6 18.5 reduce-scatter.1

commit v2 on v1

--- a/solution.py
+++ b/solution.py
@@ -15,6 +15,7 @@
 F32 = jnp.float32
 BF16 = jnp.bfloat16
 LOG2E = 1.4426950408889634
+SEND = 8
 
 
 def pixel_tables(tiles):
@@ -57,16 +58,37 @@
 def dot(a, b):
     return jnp.dot(a, b, preferred_element_type=F32)
 
+def selection(count):
+    row = lax.broadcasted_iota(jnp.int32, (128, count), 0)
+    column = lax.broadcasted_iota(jnp.int32, (128, count), 1)
+    select = jnp.where(row == column // SEND, 1.0, 0.0).astype(BF16)
+    return select, row // 16 == column % SEND
+
+
+def to_rows(parts, select, mask):
+    total = None
+    for part in parts:
+        tiled = jnp.where(mask, jnp.concatenate([part.astype(F32)] * SEND, 0), 0.0).astype(BF16)
+        term = lax.dot_general(select, tiled, (((1,), (1,)), ((), ())), preferred_element_type=F32)
+        total = term if total is None else total + term
+    return total
+
+
+def from_rows(x, select, mask):
+    total = sum(dot(part, select) for part in pieces(x.T, 3))
+    total = jnp.where(mask, total, 0.0)
+    return sum(total[16 * p : 16 * p + 16, :] for p in range(SEND))
+
 
 def tiles_kernel(
     lists_ref, lengths_ref, base_ref,
-    geo_ref, feat_ref, decoder_ref, teacher_ref, images_ref, basis_ref, moments_ref, order_ref,
-    geo_grad_ref, feat_grad_ref, decoder_grad_ref,
-    rows, columns, feat_t, alphas, weights, weights_b, terms, right, small,
+    geo_rows_ref, feat_ref, decoder_ref, teacher_ref, images_ref, basis_ref, moments_ref, order_ref,
+    geo_grad_rows_ref, feat_grad_ref, decoder_tiles_ref,
+    geo_ref, geo_grad_ref, decoder_grad_ref, rows, columns, feat_t, alphas, weights, weights_b, terms, right, small,
 ):
     tile = pl.program_id(0)
     tiles = pl.num_programs(0)
-    count = geo_ref.shape[1]
+    count = feat_ref.shape[0]
     nblocks = count // BLK
 
     def parameters():
@@ -80,6 +102,7 @@
 
     @pl.when(tile == 0)
     def _():
+        geo_ref[...] = from_rows(geo_rows_ref[...], *selection(count))
         rows[...] = jnp.zeros_like(rows)
         feat_grad_ref[...] = jnp.zeros_like(feat_grad_ref)
         decoder_grad_ref[...] = jnp.zeros_like(decoder_grad_ref)
@@ -205,6 +228,13 @@
         geo_grad_ref[4:5, :] = -dxy * scale * (1.0 - slope * slope)
         geo_grad_ref[5:6, :] = s0 / (1.0 + jnp.exp(geo_ref[5:6, :]))
         geo_grad_ref[6:9, :] = rows[0:3, :] + rows[3:6, :] + rows[9:12, :]
+        geo_grad_ref[9:16, :] = jnp.zeros((7, count), F32)
+        geo_grad_rows_ref[...] = to_rows(pieces(geo_grad_ref[...], 3), *selection(count))
+        for row in range(FEAT // 8):
+            for lane in range(CT // 128):
+                decoder_tiles_ref[row * (CT // 128) + lane] = decoder_grad_ref[
+                    8 * row : 8 * row + 8, 128 * lane : 128 * lane + 128
+                ]
 
 
 def device_terms(recv_geo, recv_feat, decoder, teacher, images, lists, lengths, shard_index):
@@ -222,20 +252,23 @@
         grid=(tiles,),
         in_specs=[
             smem, smem, smem,
-            whole((9, count)), whole((count, FEAT)), whole((FEAT, CT)),
+            whole((128, 128)), whole((count, FEAT)), whole((FEAT, CT)),
             pl.BlockSpec((PIX, CT), lambda k: (k, 0)),
             pl.BlockSpec((3, PIX), lambda k: (0, k)),
             pl.BlockSpec((1, 128, PIX), lambda k: (k, 0, 0)),
             pl.BlockSpec((1, PIX, 128), lambda k: (k, 0, 0)),
             whole((2, BLK, 2 * BLK)),
         ],
-        out_specs=[whole((9, count)), whole((count, FEAT)), whole((FEAT, CT))],
+        out_specs=[whole((128, 128)), whole((count, FEAT)), whole((FEAT * CT // 1024, 8, 128))],
         out_shape=[
-            jax.ShapeDtypeStruct((9, count), F32),
+            jax.ShapeDtypeStruct((128, 128), F32),
             jax.ShapeDtypeStruct((count, FEAT), F32),
-            jax.ShapeDtypeStruct((FEAT, CT), F32),
+            jax.ShapeDtypeStruct((FEAT * CT // 1024, 8, 128), F32),
         ],
         scratch_shapes=[
+            pltpu.VMEM((16, count), F32),
+            pltpu.VMEM((16, count), F32),
+            pltpu.VMEM((FEAT, CT), F32),
             pltpu.VMEM((128, count), F32),
             pltpu.VMEM((count, 2 * BLK), BF16),
             pltpu.VMEM((count // BLK, FEAT + 32, BLK), BF16),
@@ -253,23 +286,358 @@
     return dec, geo, feat
 
 
+Y, Z, C, X = 8, 8, 2, 4
+GROUP = (Y, Z, C)
+
+
+def place():
+    index = lax.axis_index("gs")
+    return index // (Z * C), (index // C) % Z, index % C, lax.axis_index("view")
+
+
+def gs_of(y, z, c):
+    return (y * Z + z) * C + c
+
+
+def loop(start, stop, body):
+    def step(i, carry):
+        body(i)
+        return carry
+
+    lax.fori_loop(start, stop, step, 0)
+
+
+def greet(targets):
+    barrier = pltpu.get_barrier_semaphore()
+    for count, target in targets:
+        loop(0, count, lambda i: pl.semaphore_signal(
+            barrier, inc=1, device_id=target(i), device_id_type=pl.DeviceIdType.MESH))
+    pl.semaphore_wait(barrier, sum(count for count, _ in targets))
+
+
+def line_targets():
+    y, z, c, _ = place()
+    return [
+        (Y - 1, lambda i: {"gs": gs_of((y + 1 + i) % Y, z, c)}),
+        (Z - 1, lambda i: {"gs": gs_of(y, (z + 1 + i) % Z, c)}),
+        (Z, lambda i: {"gs": gs_of(y, i, 1 - c)}),
+    ]
+
+
+def remote(src, dst, sems, mine, theirs, target):
+    return pltpu.make_async_remote_copy(
+        src_ref=src, dst_ref=dst, send_sem=sems.at[0, mine], recv_sem=sems.at[1, theirs],
+        device_id=target, device_id_type=pl.DeviceIdType.MESH,
+    )
+
+
+class Exchange:
+    def __init__(self, pairs, sems):
+        self.pairs = pairs
+        self.sems = sems
+
+    def copies(self, stage, i):
+        y, z, c, _ = place()
+        out = []
+        for n, (send, hop_a, hop_b, recv) in enumerate(self.pairs):
+            sems = self.sems.at[4 * n + stage]
+            if stage == 0:
+                to = (y + i) % Y
+                out.append(remote(send.at[to, :, c], hop_a.at[y], sems, i, i, {"gs": gs_of(to, z, c)}))
+            elif stage == 1:
+                to = (z + i) % Z
+                out.append(remote(send.at[:, to, 1 - c], hop_b.at[z], sems, i, i, {"gs": gs_of(y, to, 1 - c)}))
+            elif stage == 2:
+                to = (z + i) % Z
+                out.append(remote(hop_a.at[:, to], recv.at[:, z, c], sems, i, i, {"gs": gs_of(y, to, c)}))
+            else:
+                to = (y + i) % Y
+                out.append(remote(hop_b.at[:, to], recv.at[y, :, 1 - c], sems, i, i, {"gs": gs_of(to, z, c)}))
+        return out
+
+    def first(self, stage):
+        return 0 if stage == 1 else 1
+
+    def start(self, stage):
+        def body(i):
+            for copy in self.copies(stage, i):
+                copy.start()
+
+        loop(self.first(stage), 8, body)
+
+    def arrive(self, stage):
+        def body(i):
+            for copy in self.copies(stage, i):
+                copy.wait_recv()
+
+        loop(self.first(stage), 8, body)
+
+    def sent(self, stage):
+        def body(i):
+            for copy in self.copies(stage, i):
+                copy.wait_send()
+
+        loop(self.first(stage), 8, body)
+
+    def keep_first(self):
+        y, z, c, _ = place()
+        for send, hop_a, hop_b, recv in self.pairs:
+            hop_a[y] = send[y, :, c]
+
+    def keep_a(self):
+        y, z, c, _ = place()
+        for send, hop_a, hop_b, recv in self.pairs:
+            recv[:, z, c] = hop_a[:, z]
+
+    def keep_b(self):
+        y, z, c, _ = place()
+        for send, hop_a, hop_b, recv in self.pairs:
+            recv[y, :, 1 - c] = hop_b[:, y]
+
+
+def forward_kernel(
+    order_ref, feat_ref, geo_ref, feat_out, geo_out,
+    source, gathered, send_f, send_g, a_f, a_g, b_f, b_g, sems,
+):
+    count = feat_ref.shape[0]
+    greet(line_targets())
+    for n in range(count // BLK):
+        span = slice(n * BLK, (n + 1) * BLK)
+        source[0:FEAT, span] = feat_ref[span, :].astype(F32).T.astype(BF16)
+    padded = jnp.concatenate([geo_ref[...], jnp.zeros((7, count), F32)], 0)
+    for index, part in enumerate(pieces(padded, 3)):
+        source[FEAT + 16 * index : FEAT + 16 * index + 16, :] = part
+    step = 256
+    for n in range(count // step):
+        span = slice(n * step, (n + 1) * step)
+        row = lax.broadcasted_iota(jnp.int32, (count, step), 0)
+        onehot = jnp.where(row == order_ref[:, span], 1.0, 0.0).astype(BF16)
+        picked = dot(source[...], onehot)
+        block = picked[0:FEAT, :].T.reshape(step // (Z * C * SEND), Z, C, SEND, FEAT).astype(BF16)
+        send_f[n * 2 : n * 2 + 2] = block
+        gathered[:, span] = picked[FEAT : FEAT + 48, :]
+    parts = [gathered[16 * i : 16 * i + 16, :] for i in range(3)]
+    rows = to_rows(parts, *selection(count))
+    for d in range(Y * Z * C):
+        send_g[d // (Z * C), (d // C) % Z, d % C] = rows[d : d + 1, :]
+
+    exchange = Exchange([(send_f, a_f, b_f, feat_out), (send_g, a_g, b_g, geo_out)], sems)
+    exchange.start(0)
+    exchange.start(1)
+    exchange.keep_first()
+    exchange.arrive(0)
+    exchange.start(2)
+    exchange.keep_a()
+    exchange.arrive(1)
+    exchange.start(3)
+    exchange.keep_b()
+    exchange.arrive(2)
+    exchange.arrive(3)
+    for stage in range(4):
+        exchange.sent(stage)
+
+
+def exchange_buffers(dtype):
+    return [
+        pltpu.VMEM((Y, Z, SEND, FEAT), dtype), pltpu.VMEM((Y, Z, 1, 128), F32),
+        pltpu.VMEM((Z, Y, SEND, FEAT), dtype), pltpu.VMEM((Z, Y, 1, 128), F32),
+    ]
+
+
+def forward_exchange(order, features, geometry):
+    count = features.shape[0]
+    vmem = pl.BlockSpec(memory_space=pltpu.VMEM)
+    return pl.pallas_call(
+        forward_kernel,
+        in_specs=[vmem] * 3,
+        out_specs=[vmem] * 2,
+        out_shape=[
+            jax.ShapeDtypeStruct((*GROUP, SEND, FEAT), BF16),
+            jax.ShapeDtypeStruct((*GROUP, 1, 128), F32),
+        ],
+        scratch_shapes=[
+            pltpu.VMEM((FEAT + 48, count), BF16),
+            pltpu.VMEM((48, count), F32),
+            pltpu.VMEM((*GROUP, SEND, FEAT), BF16),
+            pltpu.VMEM((*GROUP, 1, 128), F32),
+            *exchange_buffers(BF16),
+            pltpu.SemaphoreType.DMA((8, 2, 8)),
+        ],
+        compiler_params=pltpu.CompilerParams(collective_id=0, has_side_effects=True),
+        name="forward_exchange",
+    )(order, features, geometry)
+
+
+def return_kernel(
+    scale, order_ref, send_f, send_g, dec_ref, feat_out, geo_out, dec_out,
+    a_f, a_g, b_f, b_g, recv_f, recv_g, geo_rows, returned, shares, view_in,
+    d1, p1, d2, p2, d3, p3, d4, d5, sems, sum_sems, view_sems,
+):
+    y, z, c, x = place()
+    count = order_ref.shape[1]
+    corner = x * C + c
+
+    def xc(i):
+        to = (corner + i) % (X * C)
+        return to, {"gs": gs_of(y, z, to % C), "view": to // C}
+
+    greet(line_targets() + [
+        (X - 1, lambda i: {"gs": gs_of(y, z, c), "view": (x + 1 + i) % X}),
+        (X - 1, lambda i: {"gs": gs_of(y, z, 1 - c), "view": (x + 1 + i) % X}),
+    ])
+
+    def sum_copy(stage, i):
+        sems = sum_sems.at[stage]
+        if stage == 0:
+            to, target = xc(i)
+            return remote(dec_ref.at[pl.ds(to * Z, Z)], d1.at[corner], sems, i, i, target)
+        if stage == 1:
+            to = (z + i) % Z
+            return remote(p1.at[to], d2.at[z], sems, i, i, {"gs": gs_of(y, to, c)})
+        if stage == 2:
+            to = (y + i) % Y
+            return remote(p2, d3.at[y], sems, i, i, {"gs": gs_of(to, z, c)})
+        if stage == 3:
+            to = (z + i) % Z
+            return remote(p3, d4.at[z], sems, i, i, {"gs": gs_of(y, to, c)})
+        to, target = xc(i)
+        return remote(d4, d5.at[corner], sems, i, i, target)
+
+    def sum_start(stage):
+        loop(1, 8, lambda i: sum_copy(stage, i).start())
+
+    def sum_arrive(stage):
+        loop(1, 8, lambda i: sum_copy(stage, i).wait_recv())
+
+    exchange = Exchange([(send_f, a_f, b_f, recv_f), (send_g, a_g, b_g, recv_g)], sems)
+    sum_start(0)
+    exchange.start(0)
+    exchange.start(1)
+    exchange.keep_first()
+    d1[corner] = dec_ref[pl.ds(corner * Z, Z)]
+    sum_arrive(0)
+    p1[...] = sum(d1[i] for i in range(X * C))
+    sum_start(1)
+    d2[z] = p1[z]
+    sum_arrive(1)
+    p2[...] = sum(d2[i] for i in range(Z))
+    sum_start(2)
+    d3[y] = p2[...]
+    exchange.arrive(0)
+    exchange.start(2)
+    exchange.keep_a()
+    exchange.arrive(1)
+    exchange.start(3)
+    exchange.keep_b()
+    sum_arrive(2)
+    p3[...] = sum(d3[i] for i in range(Y)) * scale
+    sum_start(3)
+    d4[z] = p3[...]
+    sum_arrive(3)
+    sum_start(4)
+    d5[corner] = d4[...]
+    exchange.arrive(2)
+    exchange.arrive(3)
+
+    for d in range(Y * Z * C):
+        geo_rows[d : d + 1, :] = recv_g[d // (Z * C), (d // C) % Z, d % C]
+    geo = from_rows(geo_rows[...], *selection(count))
+    geo_parts = jnp.concatenate([part.astype(F32) for part in pieces(geo, 3)], 0).astype(BF16)
+    for n in range(Y):
+        high, low = pieces(recv_f[n].reshape(Z * C * SEND, FEAT), 2)
+        span = slice(n * Z * C * SEND, (n + 1) * Z * C * SEND)
+        returned[span, 0:FEAT] = high
+        returned[span, FEAT : 2 * FEAT] = low
+
+    quarter = count // X
+
+    def view_copy(i):
+        return remote(
+            shares.at[i], view_in.at[x], view_sems, i, i, {"gs": gs_of(y, z, c), "view": (x + i) % X}
+        )
+
+    for i in (1, 2, 3, 0):
+        start = pl.multiple_of(((x + i) % X) * quarter, quarter)
+        row = lax.broadcasted_iota(jnp.int32, (quarter, count), 0) + start
+        onehot = jnp.where(row == order_ref[...], 1.0, 0.0).astype(BF16)
+        both = dot(onehot, returned[...])
+        share = both[:, 0:FEAT] + both[:, FEAT : 2 * FEAT]
+        if i:
+            shares[i] = share
+            view_copy(i).start()
+        else:
+            view_in[x] = share
+        own = lax.dot_general(geo_parts, onehot, (((1,), (1,)), ((), ())), preferred_element_type=F32)
+        own = own[0:16] + own[16:32] + own[32:48]
+        geo_out[:, pl.ds(start, quarter)] = own[0:9]
+
+    sum_arrive(4)
+    for row in range(FEAT // 8):
+        for lane in range(CT // 128):
+            n = row * (CT // 128) + lane
+            dec_out[8 * row : 8 * row + 8, 128 * lane : 128 * lane + 128] = d5[n // Z, n % Z]
+    for i in (1, 2, 3):
+        view_copy(i).wait_recv()
+    feat_out[...] = view_in[0] + view_in[1] + view_in[2] + view_in[3]
+    for i in (1, 2, 3):
+        view_copy(i).wait_send()
+    for stage in range(5):
+        loop(1, 8, lambda i: sum_copy(stage, i).wait_send())
+    for stage in range(4):
+        exchange.sent(stage)
+
+
+def return_exchange(order, feat, geo, dec, scale):
+    count = order.shape[1]
+    quarter = count // X
+    vmem = pl.BlockSpec(memory_space=pltpu.VMEM)
+    tile = (8, 128)
+    return pl.pallas_call(
+        functools.partial(return_kernel, scale),
+        in_specs=[vmem] * 4,
+        out_specs=[vmem] * 3,
+        out_shape=[
+            jax.ShapeDtypeStruct((quarter, FEAT), F32),
+            jax.ShapeDtypeStruct((9, count), F32),
+            jax.ShapeDtypeStruct((FEAT, CT), F32),
+        ],
+        scratch_shapes=[
+            *exchange_buffers(F32),
+            pltpu.VMEM((*GROUP, SEND, FEAT), F32),
+            pltpu.VMEM((*GROUP, 1, 128), F32),
+            pltpu.VMEM((128, 128), F32),
+            pltpu.VMEM((count, 2 * FEAT), BF16),
+            pltpu.VMEM((X, quarter, FEAT), F32),
+            pltpu.VMEM((X, quarter, FEAT), F32),
+            pltpu.VMEM((X * C, Z, *tile), F32),
+            pltpu.VMEM((Z, *tile), F32),
+            pltpu.VMEM((Z, *tile), F32),
+            pltpu.VMEM(tile, F32),
+            pltpu.VMEM((Y, *tile), F32),
+            pltpu.VMEM(tile, F32),
+            pltpu.VMEM((Z, *tile), F32),
+            pltpu.VMEM((X * C, Z, *tile), F32),
+            pltpu.SemaphoreType.DMA((8, 2, 8)),
+            pltpu.SemaphoreType.DMA((5, 2, 8)),
+            pltpu.SemaphoreType.DMA((2, X)),
+        ],
+        compiler_params=pltpu.CompilerParams(collective_id=1, has_side_effects=True),
+        name="return_exchange",
+    )(order, feat, geo, dec)
+
+
 def on_device(features, geometry, decoder, teacher, images, send_index, tile_lists, tile_lengths):
-    send_order = send_index[0, 0]
+    order = send_index[0]
     shard_index = lax.axis_index("gs")
-    geo_send = jnp.take(geometry[0], send_order, axis=1)
-    recv_geo = lax.all_to_all(geo_send, "gs", split_axis=1, concat_axis=1, tiled=True)
-    feat_send = jnp.take(features, send_order, axis=0)
-    recv_feat = lax.all_to_all(feat_send, "gs", split_axis=0, concat_axis=0, tiled=True)
-    decoder_sum, geo_acc, feat_acc = device_terms(
-        recv_geo, recv_feat, decoder, teacher[0], images[0], tile_lists[0], tile_lengths[0], shard_index
+    recv_feat, recv_geo = forward_exchange(order, features, geometry[0])
+    pixel_total = lax.axis_size("gs") * lax.axis_size("view") * tile_lists.shape[1] * PIX
+    dec, geo, feat = device_terms(
+        recv_geo.reshape(128, 128), recv_feat.reshape(-1, FEAT), decoder, teacher[0], images[0],
+        tile_lists[0], tile_lengths[0], shard_index,
     )
-    returned_geo = lax.all_to_all(geo_acc, "gs", split_axis=1, concat_axis=1, tiled=True)
-    returned_feat = lax.all_to_all(feat_acc, "gs", split_axis=0, concat_axis=0, tiled=True)
-    geo_own = jnp.zeros_like(returned_geo).at[:, send_order].set(returned_geo)
-    feat_own = jnp.zeros_like(returned_feat).at[send_order].set(returned_feat)
-    feature_grad = lax.psum_scatter(feat_own, "view", scatter_dimension=0, tiled=True)
-    pixel_total = lax.axis_size("gs") * lax.axis_size("view") * tile_lists.shape[1] * PIX
-    decoder_grad = lax.psum(decoder_sum, ("gs", "view")) * (1.0 / math.sqrt(pixel_total))
+    feature_grad, geo_own, decoder_grad = return_exchange(
+        order, feat.reshape(*GROUP, SEND, FEAT), geo.reshape(*GROUP, 1, 128), dec, 1.0 / math.sqrt(pixel_total)
+    )
     return (feature_grad, geo_own[None], decoder_grad)
 
 

time: 396 us -> 103 us (0.26)
  waiting for transfers between devices: 271 us -> 0 us
  Pallas kernels: 24 us -> 96.6 us
  starting transfers between devices: 32.8 us -> 0 us
  blocking collectives: 26.2 us -> 0 us
  between operations: 15.6 us -> 0.71 us
  local copies, waits for them, and re-layouts: 19.4 us -> 5.08 us
  other arithmetic: 5.68 us -> 0.65 us
    psum x1 -> x0, waiting for transfers between devices: 225 us -> none  [on_device(): lax.psum(decoder_sum, ('gs', 'view')) * (1.0 / math.sqrt(pixel_total))]
    pallas_call x0 -> x2, Pallas kernels: none -> 71.9 us  [the longest x1 40.9 us: return_exchange(): pl.pallas_call(functools.partial(return_kernel, scale), in_specs=[vmem] *...]
    all_to_all x3 -> x0, waiting for transfers between devices: 45.5 us -> none  [the longest x1 18.6 us: on_device(): lax.all_to_all(feat_acc, 'gs', split_axis=0, concat_axis=0, tiled=True)]
    all_to_all x3 -> x0, starting transfers between devices: 32.6 us -> none  [the longest x1 18.4 us: on_device(): lax.all_to_all(geo_send, 'gs', split_axis=1, concat_axis=1, tiled=True)]
    all_to_all x1 -> x0, blocking collectives: 26.2 us -> none  [on_device(): lax.all_to_all(geo_acc, 'gs', split_axis=1, concat_axis=1, tiled=True)]
    scatter x2 -> x0, local copies, waits for them, and re-layouts: 7.14 us -> none  [the longest x1 3.89 us: on_device(): feat_own = jnp.zeros_like(returned_feat).at[send_order].set(returned_feat)]
    gather x2 -> x0, local copies, waits for them, and re-layouts: 6.02 us -> none  [the longest x1 3.21 us: on_device(): feat_send = jnp.take(features, send_order, axis=0)]
  transfers between devices with their start and end apart: 5 -> 0, of which waited for: 4 -> 0; matrix products, arithmetic and copies ran while one was open for 4% -> 0% of each run, Pallas kernels for 0% -> 0%
where the time goes in v2:
time: 103 us
  Pallas kernels  96.6 us (94%)
  local copies, waits for them, and re-layouts  5.08 us (5%)
    pallas_call x1, Pallas kernels, return_exchange(): pl.pallas_call(functools.partial(return_kernel, scale), in_specs=[vmem] *...  40.9 us
    pallas_call x1, Pallas kernels, forward_exchange(): pl.pallas_call(forward_kernel, in_specs=[vmem] * 3, out_specs=[vmem] * 2,...  30.9 us
    pallas_call x1, Pallas kernels, device_terms(): pl.pallas_call(tiles_kernel, grid=(tiles,), in_specs=[smem, smem, smem, w...  24.8 us
    unnamed x11, local copies, waits for them, and re-layouts  5.08 us

profile of v2, /device:TPU:1, one launch (start us, length us, event | category | flops | bytes accessed | tf_op | source)
XLA Modules:
  0.0 103.1 jit_solution(8554611667999987039)
XLA Ops:
  0.6 0.0 copy-start.2
  0.6 0.0 copy-start.1
  0.7 0.6 add_convert_fusion.base_ref
  1.3 0.0 copy-done.2
  1.3 0.6 copy.20
  2.0 0.0 copy-done.1
  2.0 0.6 copy.19
  2.6 30.9 %forward_exchange.1 = (bf16[8,8,2,8,128]{4,3,2,1,0:T(8,128)(2,1)}, f32[8,8,2,1,128]{4,3,2,1,0:T(1,128)}) custom-call(s32[1,1024]{1,0:T(1,128)} %bitcast.25, bf16[1024,128]{1,0:T(8,128)(2,1)} %feat_ref.1, f32[9,1024]{1,0:T(8,128)} %bitcast.20), custom_call_target="tpu_custom_call" | custom-call | tf_op jit(solution)/shard_map/forward_exchange/pallas_call | solution.py:450
  33.5 24.8 %tiles.1 = (f32[128,128]{1,0:T(8,128)}, f32[1024,128]{1,0:T(8,128)}, f32[64,8,128]{2,1,0:T(8,128)}) custom-call(s32[4,8]{1,0:T(4,128)} %bitcast.27, s32[4]{0:T(128)} %bitcast.28, f32[2]{0:T(128)} %add_convert_fusion.base_ref, f32[128,128]{1,0:T(8,128)} %bitcast.22, bf16[1024,128]{1,0:T(8,128)(2,1)} %bitcast.19, bf16[128,512]{1,0:T(8,128)(2,1)} %decoder_ref.1, ...), custom_call_target="tpu_custom_call" | custom-call | tf_op jit(solution)/shard_map/tiles/pallas_call | solution.py:250
  58.3 40.9 %return_exchange.1 = (f32[256,128]{1,0:T(8,128)}, f32[9,1024]{1,0:T(8,128)}, f32[128,512]{1,0:T(8,128)}) custom-call(s32[1,1024]{1,0:T(1,128)} %bitcast.26, f32[8,8,2,8,128]{4,3,2,1,0:T(8,128)} %bitcast.18, f32[8,8,2,1,128]{4,3,2,1,0:T(1,128)} %bitcast.24, f32[64,8,128]{2,1,0:T(8,128)} %get-tuple-element.15.dec_ref), custom_call_target="tpu_custom_call" | custom-call | tf_op jit(solution)/shard_map/return_exchange/pallas_call | solution.py:595
  99.2 0.0 copy-start
  99.2 1.5 %copy.14 = f32[1,9,1024]{2,0,1:T(1,128)} copy(f32[1,9,1024]{2,1,0:T(8,128)} %bitcast.23) | data formatting | bytes 73728
  100.8 1.6 %copy.23 = f32[256,128]{1,0:T(8,128)} copy(f32[256,128]{1,0:T(8,128)} %get-tuple-element.25) | data formatting | bytes 262144
  102.4 0.0 copy-done
  102.4 0.7 copy.24
Async XLA Ops:
  0.6 0.7 copy-start.2
  0.6 1.3 %copy-start.1 = (f32[1,9,1024]{2,0,1:T(1,128)S(1)}, f32[1,9,1024]{2,0,1:T(1,128)}, u32[]{:S(2)}) copy-start(f32[1,9,1024]{2,0,1:T(1,128)} %param.12) | copy-start | bytes 110596
  99.2 3.1 %copy-start = (f32[128,512]{1,0:T(8,128)S(1)}, f32[128,512]{1,0:T(8,128)}, u32[]{:S(2)}) copy-start(f32[128,512]{1,0:T(8,128)} %get-tuple-element.27) | copy-start | bytes 786436

commit v3 on v0

v3 whole, which is shorter than its diff:
```python
import functools
import math

import jax
import jax.numpy as jnp
import numpy as np
from jax import lax
from jax.experimental import pallas as pl
from jax.experimental.pallas import tpu as pltpu
from jax.sharding import PartitionSpec as P

FEAT = 128
CT = 512
TS = 16
BLK = 128
LIST = 8
PIX = TS * TS
SEND = 8
Y, Z, C, X = 8, 8, 2, 4
GROUP = (Y, Z, C)
F32 = jnp.float32
BF16 = jnp.bfloat16
LOG2E = 1.4426950408889634


def pixel_tables(tiles):
    q = np.arange(PIX)
    basis = np.zeros((tiles, 128, PIX), np.float32)
    moments = np.zeros((tiles, PIX, 128), np.float32)
    for k in range(tiles):
        px = TS * (k % 2) + q % TS + 0.5 - TS
        py = TS * (k // 2) + q // TS + 0.5 - TS
        rows = [np.ones(PIX), px, py]
        for square in (px * px, px * py, py * py):
            high = square.astype(jnp.bfloat16).astype(np.float64)
            rows += [high, square - high]
        row = 32
        for index, values in enumerate(rows):
            basis[k, row : row + 3] = values
            row += 3
            moments[k, :, 32 + index] = values
    return basis.astype(jnp.bfloat16), moments.astype(jnp.bfloat16)


def order_tables():
    i = np.arange(BLK)
    before = (i[None, :] < i[:, None]).astype(np.float32)
    after = (i[None, :] > i[:, None]).astype(np.float32)
    return np.stack(
        [np.concatenate([before, before], 1), np.concatenate([after, after], 1)]
    ).astype(jnp.bfloat16)


def pieces(x, count):
    parts = []
    for _ in range(count):
        part = x.astype(BF16)
        parts.append(part)
        x = x - part.astype(F32)
    return parts


def dot(a, b):
    return jnp.dot(a, b, preferred_element_type=F32)


def dot_t(a, b):
    return lax.dot_general(a, b, (((1,), (1,)), ((), ())), preferred_element_type=F32)


def to_rows(parts, select, mask):
    total = None
    for part in parts:
        tiled = (jnp.concatenate([part.astype(F32)] * SEND, 0) * mask).astype(BF16)
        term = dot_t(select, tiled)
        total = term if total is None else total + term
    return total


def from_rows(x, select, mask):
    total = sum(dot(part, select) for part in pieces(x.T, 3)) * mask
    return sum(total[16 * p : 16 * p + 16, :] for p in range(SEND))


def place():
    index = lax.axis_index("gs")
    return index // (Z * C), (index // C) % Z, index % C, lax.axis_index("view")


def gs_of(y, z, c):
    return (y * Z + z) * C + c


def loop(start, stop, body):
    def step(i, carry):
        body(i)
        return carry

    lax.fori_loop(start, stop, step, 0)


def remote(src, dst, sems, i, target):
    return pltpu.make_async_remote_copy(
        src_ref=src, dst_ref=dst, send_sem=sems.at[0, i], recv_sem=sems.at[1, i],
        device_id=target, device_id_type=pl.DeviceIdType.MESH,
    )


class Exchange:
    def __init__(self, pairs, sems):
        self.pairs = pairs
        self.sems = sems

    def copies(self, stage, i):
        y, z, c, _ = place()
        out = []
        for n, (send, hop_a, hop_b, recv) in enumerate(self.pairs):
            sems = self.sems.at[4 * n + stage]
            if stage == 0:
                to = (y + i) % Y
                out.append(remote(send.at[to, :, c], hop_a.at[y], sems, i, {"gs": gs_of(to, z, c)}))
            elif stage == 1:
                to = (z + i) % Z
                out.append(remote(send.at[:, to, 1 - c], hop_b.at[z], sems, i, {"gs": gs_of(y, to, 1 - c)}))
            elif stage == 2:
                to = (z + i) % Z
                out.append(remote(hop_a.at[:, to], recv.at[:, z, c], sems, i, {"gs": gs_of(y, to, c)}))
            else:
                to = (y + i) % Y
                out.append(remote(hop_b.at[:, to], recv.at[y, :, 1 - c], sems, i, {"gs": gs_of(to, z, c)}))
        return out

    def each(self, stage, act):
        def body(i):
            for copy in self.copies(stage, i):
                act(copy)

        loop(0 if stage == 1 else 1, 8, body)

    def start(self, stage):
        self.each(stage, lambda copy: copy.start())

    def arrive(self, stage):
        self.each(stage, lambda copy: copy.wait_recv())

    def sent(self):
        for stage in range(4):
            self.each(stage, lambda copy: copy.wait_send())

    def keep_first(self):
        y, z, c, _ = place()
        for send, hop_a, hop_b, recv in self.pairs:
            hop_a[y] = send[y, :, c]

    def keep_a(self):
        y, z, c, _ = place()
        for send, hop_a, hop_b, recv in self.pairs:
            recv[:, z, c] = hop_a[:, z]

    def keep_b(self):
        y, z, c, _ = place()
        for send, hop_a, hop_b, recv in self.pairs:
            recv[y, :, 1 - c] = hop_b[:, y]


def step_kernel(
    scale, lists_ref, lengths_ref, order_ref, feat_ref, geo_in_ref, decoder_ref, images_ref,
    teacher_hbm, basis_hbm, moments_hbm, tables_hbm,
    feat_out, geo_out, dec_out,
    teacher_ref, basis_ref, moments_ref, tables_ref, load_sems,
    onehot, select, mask, source, gathered,
    fsend_f, fsend_g, fa_f, fa_g, fb_f, fb_g, frecv_f, frecv_g, forward_sems,
    geo_rows, geo, geo_grad, rows, columns, feat_t, alphas, weights, weights_b, inners, values, bias, totals, carry,
    terms, right, acc, dec,
    rsend_f, rsend_g, ra_f, ra_g, rb_f, rb_g, rrecv_f, rrecv_g, return_sems,
    dec_tiles, d1, p1, d2, p2, d3, p3, d4, d5, sum_sems,
    returned, shares, view_in, view_sems,
):
    y, z, c, x = place()
    count = feat_ref.shape[0]
    tiles = lists_ref.shape[0]
    nblocks = count // BLK
    corner = x * C + c

    loads = [
        pltpu.make_async_copy(src, dst, load_sems.at[n])
        for n, (src, dst) in enumerate((
            (teacher_hbm, teacher_ref), (basis_hbm, basis_ref), (moments_hbm, moments_ref), (tables_hbm, tables_ref)
        ))
    ]
    for load in loads:
        load.start()

    barrier = pltpu.get_barrier_semaphore()

    def greet(start, stop, target):
        loop(start, stop, lambda i: pl.semaphore_signal(
            barrier, inc=1, device_id=target(i), device_id_type=pl.DeviceIdType.MESH))

    greet(1, Y, lambda i: {"gs": gs_of((y + i) % Y, z, c)})
    greet(1, Z, lambda i: {"gs": gs_of(y, (z + i) % Z, c)})
    greet(0, Z, lambda i: {"gs": gs_of(y, (z + i) % Z, 1 - c)})
    greet(1, X, lambda i: {"gs": gs_of(y, z, c), "view": (x + i) % X})
    greet(1, X, lambda i: {"gs": gs_of(y, z, 1 - c), "view": (x + i) % X})

    row = lax.broadcasted_iota(jnp.int32, (128, count), 0)
    column = lax.broadcasted_iota(jnp.int32, (128, count), 1)
    select[...] = jnp.where(row == jnp.right_shift(column, 3), 1.0, 0.0).astype(BF16)
    mask[...] = jnp.where(jnp.right_shift(row, 4) == jnp.bitwise_and(column, 7), 1.0, 0.0)
    for n in range(nblocks):
        span = slice(n * BLK, (n + 1) * BLK)
        source[0:FEAT, span] = feat_ref[span, :].astype(F32).T.astype(BF16)
    padded = jnp.concatenate([geo_in_ref[n] for n in range(9)] + [jnp.zeros((7, count), F32)], 0)
    for index, part in enumerate(pieces(padded, 3)):
        source[FEAT + 16 * index : FEAT + 16 * index + 16, :] = part
    step = 2 * Z * C * SEND
    for n in range(count // step):
        span = slice(n * step, (n + 1) * step)
        row = lax.broadcasted_iota(jnp.int32, (count, step), 0)
        hot = jnp.where(row == order_ref[:, span], 1.0, 0.0).astype(BF16)
        onehot[:, span] = hot
        picked = dot(source[...], hot)
        fsend_f[n * 2 : n * 2 + 2] = picked[0:FEAT, :].T.reshape(2, Z, C, SEND, FEAT).astype(BF16)
        gathered[:, span] = picked[FEAT : FEAT + 48, :]
    sent_rows = to_rows([gathered[16 * i : 16 * i + 16, :] for i in range(3)], select[...], mask[...])
    for d in range(Y * Z * C):
        fsend_g[d // (Z * C), (d // C) % Z, d % C] = sent_rows[d : d + 1, :]

    pl.semaphore_wait(barrier, Y - 1 + Z - 1 + Z + 2 * (X - 1))
    forward = Exchange([(fsend_f, fa_f, fb_f, frecv_f), (fsend_g, fa_g, fb_g, frecv_g)], forward_sems)
    forward.start(0)
    forward.start(1)
    forward.keep_first()
    acc[...] = jnp.zeros_like(acc)
    dec[...] = jnp.zeros_like(dec)
    rows[...] = jnp.zeros_like(rows)
    forward.arrive(0)
    forward.start(2)
    forward.keep_a()
    forward.arrive(1)
    forward.start(3)
    forward.keep_b()
    for load in loads:
        load.wait()
    forward.arrive(2)
    forward.arrive(3)

    for d in range(Y * Z * C):
        geo_rows[d : d + 1, :] = frecv_g[d // (Z * C), (d // C) % Z, d % C]
    geo[...] = from_rows(geo_rows[...], select[...], mask[...])
    shard = lax.axis_index("gs")
    center_x = (2 * TS * (shard % 30) + TS).astype(F32)
    center_y = (2 * TS * (shard // 30) + TS).astype(F32)

    def parameters():
        gx = jnp.clip(geo[0:1, :] - center_x, -4096.0, 4096.0)
        gy = jnp.clip(geo[1:2, :] - center_y, -4096.0, 4096.0)
        ca = jnp.exp(geo[2:3, :])
        cc = jnp.exp(geo[3:4, :])
        slope = jnp.tanh(geo[4:5, :])
        reach = 0.8 * jnp.exp(0.5 * (geo[2:3, :] + geo[3:4, :]))
        return gx, gy, ca, cc, slope, reach

    gx, gy, ca, cc, slope, reach = parameters()
    cb = slope * reach
    linear_x = ca * gx + cb * gy
    linear_y = cb * gx + cc * gy
    constant = -jnp.log(1.0 + jnp.exp(-geo[5:6, :])) - 0.5 * (gx * linear_x + gy * linear_y)
    at = 32
    for coefficient, repeats in (
        (constant, 1), (linear_x, 1), (linear_y, 1), (-0.5 * ca, 2), (-cb, 2), (-0.5 * cc, 2)
    ):
        parts = pieces(coefficient * LOG2E, 3)
        for _ in range(repeats):
            for part in parts:
                rows[at : at + 1, :] = part.astype(F32)
                at += 1
    high, middle, low = pieces(geo[6:9, :], 3)
    for index, part in enumerate((high, high, middle, high, middle, low)):
        rows[3 * index : 3 * index + 3, :] = part.astype(F32)
    for n in range(nblocks):
        span = slice(n * BLK, (n + 1) * BLK)
        block = frecv_f[n].astype(F32).reshape(BLK, FEAT)
        columns[span, 0:FEAT] = block.astype(BF16)
        columns[span, FEAT : 2 * FEAT] = rows[:, span].T.astype(BF16)
        feat_t[0:FEAT, span] = block.T.astype(BF16)
        feat_t[FEAT : FEAT + 32, span] = rows[0:32, span].astype(BF16)

    def xc(i):
        to = (corner + i) % (X * C)
        return to, {"gs": gs_of(y, z, to % C), "view": to // C}

    def sum_copy(stage, i):
        sems = sum_sems.at[stage]
        if stage == 0:
            to, target = xc(i)
            return remote(dec_tiles.at[to], d1.at[corner], sems, i, target)
        if stage == 1:
            to = (z + i) % Z
            return remote(p1.at[to], d2.at[z], sems, i, {"gs": gs_of(y, to, c)})
        if stage == 2:
            to = (y + i) % Y
            return remote(p2, d3.at[y], sems, i, {"gs": gs_of(to, z, c)})
        if stage == 3:
            to = (z + i) % Z
            return remote(p3, d4.at[z], sems, i, {"gs": gs_of(y, to, c)})
        to, target = xc(i)
        return remote(d4, d5.at[corner], sems, i, target)

    def sum_start(stage):
        loop(1, 8, lambda i: sum_copy(stage, i).start())

    def sum_arrive(stage):
        loop(1, 8, lambda i: sum_copy(stage, i).wait_recv())

    def tile_step(tile):
        block_i = lax.broadcasted_iota(jnp.int32, (LIST, LIST), 0)
        slot_i = lax.broadcasted_iota(jnp.int32, (LIST, LIST), 1)
        slot_col = jnp.sum(
            jnp.where(block_i == lists_ref[pl.ds(tile, 1), :], slot_i.astype(F32), 0.0), axis=1, keepdims=True
        )
        slot_row = jnp.sum(jnp.where(block_i == slot_i, slot_col, 0.0), axis=0, keepdims=True)
        earlier = jnp.where(slot_row < slot_col, 1.0, 0.0)
        later = jnp.where(slot_row > slot_col, 1.0, 0.0)
        tile_i = lax.broadcasted_iota(jnp.int32, lengths_ref.shape, 1)
        length = jnp.sum(jnp.where(tile_i == tile, lengths_ref[...].astype(F32), 0.0), axis=1, keepdims=True)
        bias[...] = jnp.broadcast_to(jnp.where(slot_col < length, 0.0, -1e30), (LIST, PIX))

        inners[...] = dot(columns[:, FEAT:], basis_ref[tile])
        for n in range(LIST):
            span = slice(n * BLK, (n + 1) * BLK)
            alpha = jnp.exp2(inners[span, :] + bias[n : n + 1, :])
            log_keep = alpha * (
                -LOG2E + alpha * (-LOG2E / 2 + alpha * (-LOG2E / 3 + alpha * (-LOG2E / 4)))
            )
            high, low = pieces(log_keep, 2)
            inner = dot(tables_ref[0], jnp.concatenate([high, low], 0))
            totals[n : n + 1, :] = inner[BLK - 1 : BLK, :] + log_keep[BLK - 1 : BLK, :]
            alphas[span, :] = alpha
            inners[span, :] = inner
        carry[...] = sum(earlier[:, n : n + 1] * totals[n : n + 1, :] for n in range(LIST))
        for n in range(LIST):
            span = slice(n * BLK, (n + 1) * BLK)
            weight = alphas[span, :] * jnp.exp2(inners[span, :] + carry[n : n + 1, :])
            weight_b, weight_low = pieces(weight, 2)
            weights[span, :] = weight
            weights_b[span, 0:PIX] = weight_b
            weights_b[span, PIX : 2 * PIX] = weight_low
        total = dot(feat_t[...], weights_b[:, 0:PIX])
        total_low = dot(feat_t[FEAT:, :], weights_b[:, PIX : 2 * PIX])

        rendered_t = total[0:FEAT, :].astype(BF16)
        color = (
            total[FEAT : FEAT + 3] + total[FEAT + 6 : FEAT + 9] + total[FEAT + 15 : FEAT + 18]
            + total_low[0:3] + total_low[6:9]
        )
        pixels = pl.ds(pl.multiple_of(tile * PIX, PIX), PIX)
        error_color = color - jnp.concatenate([images_ref[n, :, pixels] for n in range(3)], 0)
        gcolor = error_color * lax.rsqrt(error_color * error_color + 0.04)
        pred = dot(total[0:FEAT, :].T.astype(BF16), decoder_ref[...])
        error = pred - teacher_ref[pixels, :].astype(F32)
        gpred = (error * lax.rsqrt(error * error + 0.04)).astype(BF16)
        dec[...] += dot(rendered_t, gpred)

        @pl.when(tile == tiles - 1)
        def _():
            for n in range(FEAT * CT // 1024):
                row, lane = n // (CT // 128), n % (CT // 128)
                dec_tiles[n // Z, n % Z] = dec[8 * row : 8 * row + 8, 128 * lane : 128 * lane + 128]
            sum_start(0)

        terms[0:FEAT, :] = dot_t(decoder_ref[...], gpred)
        terms[FEAT:, :] = jnp.zeros_like(terms[FEAT:, :])
        for index, part in enumerate([pieces(gcolor, 3)[n] for n in (0, 1, 0, 2, 1, 0)]):
            terms[FEAT + 3 * index : FEAT + 3 * index + 3, :] = part.astype(F32)
        right[...] = terms[...].T.astype(BF16)

        values[...] = dot(columns[...], terms[...].astype(BF16))
        for n in range(LIST):
            span = slice(n * BLK, (n + 1) * BLK)
            value = values[span, :] * weights[span, :]
            high, low = pieces(value, 2)
            inner = dot(tables_ref[1], jnp.concatenate([high, low], 0))
            totals[n : n + 1, :] = inner[0:1, :] + value[0:1, :]
            values[span, :] = value
            inners[span, :] = inner
        carry[...] = sum(later[:, n : n + 1] * totals[n : n + 1, :] for n in range(LIST))
        for n in range(LIST):
            span = slice(n * BLK, (n + 1) * BLK)
            alpha = alphas[span, :]
            square = alpha * alpha
            ratio = alpha + square
            ratio = ratio + ratio * square
            ratio = ratio + ratio * (square * square)
            gexponent = values[span, :] - ratio * (inners[span, :] + carry[n : n + 1, :])
            high, low = pieces(gexponent, 2)
            weights_b[span, 2 * PIX : 3 * PIX] = high
            weights_b[span, 3 * PIX : 4 * PIX] = low
        moments = moments_ref[tile]
        acc[...] += dot(weights_b[:, 0:PIX], right[...])
        acc[:, FEAT:] += dot(weights_b[:, PIX:], jnp.concatenate([right[:, FEAT:], moments, moments], 0))

    loop(0, tiles, tile_step)

    backward = Exchange([(rsend_f, ra_f, rb_f, rrecv_f), (rsend_g, ra_g, rb_g, rrecv_g)], return_sems)
    d1[corner] = dec_tiles[corner]
    sum_arrive(0)
    p1[...] = sum(d1[i] for i in range(X * C))
    sum_start(1)
    d2[z] = p1[z]

    for n in range(nblocks):
        span = slice(n * BLK, (n + 1) * BLK)
        rsend_f[n] = acc[span, 0:FEAT].reshape(Z, C, SEND, FEAT)
        rows[:, span] = acc[span, FEAT:].T
    gx, gy, ca, cc, slope, reach = parameters()
    cb = slope * reach
    s0, sx, sy = (rows[32 + i : 33 + i, :] for i in range(3))
    sxx, sxy, syy = (rows[35 + 2 * i : 36 + 2 * i, :] + rows[36 + 2 * i : 37 + 2 * i, :] for i in range(3))
    ux = sx - gx * s0
    uy = sy - gy * s0
    dxx = sxx - 2.0 * gx * sx + gx * gx * s0
    dyy = syy - 2.0 * gy * sy + gy * gy * s0
    dxy = sxy - gx * sy - gy * sx + gx * gy * s0
    geo_grad[0:1, :] = ca * ux + cb * uy
    geo_grad[1:2, :] = cb * ux + cc * uy
    geo_grad[2:3, :] = -0.5 * (ca * dxx + cb * dxy)
    geo_grad[3:4, :] = -0.5 * (cc * dyy + cb * dxy)
    geo_grad[4:5, :] = -dxy * reach * (1.0 - slope * slope)
    geo_grad[5:6, :] = s0 / (1.0 + jnp.exp(geo[5:6, :]))
    geo_grad[6:9, :] = rows[0:3, :] + rows[3:6, :] + rows[9:12, :]
    geo_grad[9:16, :] = jnp.zeros((7, count), F32)
    back_rows = to_rows(pieces(geo_grad[...], 3), select[...], mask[...])
    for d in range(Y * Z * C):
        rsend_g[d // (Z * C), (d // C) % Z, d % C] = back_rows[d : d + 1, :]

    backward.start(0)
    backward.start(1)
    backward.keep_first()
    sum_arrive(1)
    p2[...] = sum(d2[i] for i in range(Z))
    sum_start(2)
    d3[y] = p2[...]
    backward.arrive(0)
    backward.start(2)
    backward.keep_a()
    backward.arrive(1)
    backward.start(3)
    backward.keep_b()
    sum_arrive(2)
    p3[...] = sum(d3[i] for i in range(Y)) * scale
    sum_start(3)
    d4[z] = p3[...]
    sum_arrive(3)
    sum_start(4)
    d5[corner] = d4[...]
    backward.arrive(2)
    backward.arrive(3)

    for d in range(Y * Z * C):
        geo_rows[d : d + 1, :] = rrecv_g[d // (Z * C), (d // C) % Z, d % C]
    geo_back = from_rows(geo_rows[...], select[...], mask[...])
    geo_parts = jnp.concatenate([part.astype(F32) for part in pieces(geo_back, 3)], 0).astype(BF16)
    for n in range(Y):
        high, low = pieces(rrecv_f[n].reshape(Z * C * SEND, FEAT), 2)
        span = slice(n * Z * C * SEND, (n + 1) * Z * C * SEND)
        returned[span, 0:FEAT] = high
        returned[span, FEAT : 2 * FEAT] = low
    quarter = count // X

    def view_copy(i):
        return remote(shares.at[i], view_in.at[x], view_sems, i, {"gs": gs_of(y, z, c), "view": (x + i) % X})

    for i in (2, 1, 3, 0):
        start = pl.multiple_of(((x + i) % X) * quarter, quarter)
        both = dot(onehot[pl.ds(start, quarter), :], returned[...])
        share = both[:, 0:FEAT] + both[:, FEAT : 2 * FEAT]
        if i:
            shares[i] = share
            view_copy(i).start()
        else:
            view_in[x] = share
    own = dot_t(geo_parts, onehot[...])
    own = own[0:16] + own[16:32] + own[32:48]
    for n in range(9):
        geo_out[n] = own[n : n + 1]
    sum_arrive(4)
    for n in range(FEAT * CT // 1024):
        row, lane = n // (CT // 128), n % (CT // 128)
        dec_out[8 * row : 8 * row + 8, 128 * lane : 128 * lane + 128] = d5[n // Z, n % Z]
    for i in (1, 2, 3):
        view_copy(i).wait_recv()
    feat_out[...] = view_in[0] + view_in[1] + view_in[2] + view_in[3]
    for i in (1, 2, 3):
        view_copy(i).wait_send()
    for stage in range(5):
        loop(1, 8, lambda i: sum_copy(stage, i).wait_send())
    forward.sent()
    backward.sent()


def exchange_buffers(dtype):
    geo_dtype = F32
    return [
        pltpu.VMEM((*GROUP, SEND, FEAT), dtype), pltpu.VMEM((*GROUP, 1, 128), geo_dtype),
        pltpu.VMEM((Y, Z, SEND, FEAT), dtype), pltpu.VMEM((Y, Z, 1, 128), geo_dtype),
        pltpu.VMEM((Z, Y, SEND, FEAT), dtype), pltpu.VMEM((Z, Y, 1, 128), geo_dtype),
        pltpu.VMEM((*GROUP, SEND, FEAT), dtype), pltpu.VMEM((*GROUP, 1, 128), geo_dtype),
        pltpu.SemaphoreType.DMA((8, 2, 8)),
    ]


def on_device(features, geometry, decoder, teacher, images, send_index, tile_lists, tile_lengths):
    count = features.shape[0]
    tiles = tile_lists.shape[1]
    quarter = count // X
    basis, moments = pixel_tables(tiles)
    tables = order_tables()
    scale = 1.0 / math.sqrt(lax.axis_size("gs") * lax.axis_size("view") * tiles * PIX)
    vmem = pl.BlockSpec(memory_space=pltpu.VMEM)
    hbm = pl.BlockSpec(memory_space=pl.ANY)
    tile = (8, 128)
    feature_grad, geo_own, decoder_grad = pl.pallas_call(
        functools.partial(step_kernel, scale),
        in_specs=[vmem] * 7 + [hbm] * 4,
        out_specs=[vmem] * 3,
        out_shape=[
            jax.ShapeDtypeStruct((quarter, FEAT), F32),
            jax.ShapeDtypeStruct((9, 1, count), F32),
            jax.ShapeDtypeStruct((FEAT, CT), F32),
        ],
        scratch_shapes=[
            pltpu.VMEM((tiles * PIX, CT), BF16),
            pltpu.VMEM(basis.shape, BF16),
            pltpu.VMEM(moments.shape, BF16),
            pltpu.VMEM(tables.shape, BF16),
            pltpu.SemaphoreType.DMA((4,)),
            pltpu.VMEM((count, count), BF16),
            pltpu.VMEM((128, count), BF16),
            pltpu.VMEM((128, count), F32),
            pltpu.VMEM((FEAT + 48, count), BF16),
            pltpu.VMEM((48, count), F32),
            *exchange_buffers(BF16),
            pltpu.VMEM((128, 128), F32),
            pltpu.VMEM((16, count), F32),
            pltpu.VMEM((16, count), F32),
            pltpu.VMEM((128, count), F32),
            pltpu.VMEM((count, 2 * FEAT), BF16),
            pltpu.VMEM((FEAT + 32, count), BF16),
            pltpu.VMEM((LIST * BLK, PIX), F32),
            pltpu.VMEM((LIST * BLK, PIX), F32),
            pltpu.VMEM((LIST * BLK, 4 * PIX), BF16),
            pltpu.VMEM((LIST * BLK, PIX), F32),
            pltpu.VMEM((LIST * BLK, PIX), F32),
            pltpu.VMEM((LIST, PIX), F32),
            pltpu.VMEM((LIST, PIX), F32),
            pltpu.VMEM((LIST, PIX), F32),
            pltpu.VMEM((2 * FEAT, PIX), F32),
            pltpu.VMEM((PIX, 2 * FEAT), BF16),
            pltpu.VMEM((count, 2 * FEAT), F32),
            pltpu.VMEM((FEAT, CT), F32),
            *exchange_buffers(F32),
            pltpu.VMEM((X * C, Z, *tile), F32),
            pltpu.VMEM((X * C, Z, *tile), F32),
            pltpu.VMEM((Z, *tile), F32),
            pltpu.VMEM((Z, *tile), F32),
            pltpu.VMEM(tile, F32),
            pltpu.VMEM((Y, *tile), F32),
            pltpu.VMEM(tile, F32),
            pltpu.VMEM((Z, *tile), F32),
            pltpu.VMEM((X * C, Z, *tile), F32),
            pltpu.SemaphoreType.DMA((5, 2, 8)),
            pltpu.VMEM((count, 2 * FEAT), BF16),
            pltpu.VMEM((X, quarter, FEAT), F32),
            pltpu.VMEM((X, quarter, FEAT), F32),
            pltpu.SemaphoreType.DMA((2, X)),
        ],
        compiler_params=pltpu.CompilerParams(
            collective_id=0, has_side_effects=True, vmem_limit_bytes=48 * 1024 * 1024
        ),
        name="step",
    )(
        tile_lists[0], tile_lengths, send_index[0], features, geometry.reshape(9, 1, count), decoder,
        images.reshape(3, 1, tiles * PIX), teacher[0],
        jnp.asarray(basis), jnp.asarray(moments), jnp.asarray(tables),
    )
    return (feature_grad, geo_own.reshape(1, 9, count), decoder_grad)


def solution(mesh):
    placed = (
        P("gs", None),
        P("view", None, "gs"),
        P(),
        P("view", "gs", None),
        P("view", None, "gs"),
        P("view", "gs", None),
        P("view", "gs", None),
        P("view", "gs"),
    )
    return jax.shard_map(
        on_device,
        mesh=mesh,
        in_specs=placed,
        out_specs=(P(("gs", "view"), None), P("view", None, "gs"), P()),
        check_vma=False,
    )
```

time: 613 us -> 91.7 us (0.15)
  waiting for transfers between devices: 339 us -> 0 us
  Pallas kernels: 0 us -> 80.5 us
  other arithmetic: 76.6 us -> 0 us
  local copies, waits for them, and re-layouts: 79.9 us -> 10 us
  starting transfers between devices: 39.8 us -> 0 us
  matrix products: 39.1 us -> 0 us
  loops' own time: 20.3 us -> 0 us
  between operations: 14.3 us -> 0.68 us
    psum x2 -> x0, waiting for transfers between devices: 272 us -> none  [the longest x1 224 us: on_device(): lax.psum(decoder_sum, ('gs', 'view')) * (1.0 / math.sqrt(pixel_total))]
    pallas_call x0 -> x1, Pallas kernels: none -> 80.5 us  [on_device(): pl.pallas_call(functools.partial(step_kernel, scale), in_specs=[vmem] * 7...]
    all_to_all x4 -> x0, waiting for transfers between devices: 66 us -> none  [the longest x1 19.7 us: on_device(): lax.all_to_all(geo_acc, 'gs', split_axis=1, concat_axis=1, tiled=True)]
    all_to_all x4 -> x0, starting transfers between devices: 39.7 us -> none  [the longest x1 18.4 us: on_device(): lax.all_to_all(geo_send, 'gs', split_axis=1, concat_axis=1, tiled=True)]
    dot_general x44 -> x0, matrix products: 39.1 us -> none  [the longest x12 17.3 us: composite(): jnp.einsum('pi,ci->cp', weights, tile_geo[6:9], precision=lax.Precision.H...]
    another operation x16 -> x0, other arithmetic: 25.9 us -> none  [the longest x8 22.4 us: composite(): inner = jnp.cumsum(blocked, axis=2) - blocked]
    while x265 -> x0, local copies, waits for them, and re-layouts: 21.2 us -> none
    another operation x1 -> x0, loops' own time: 20.3 us -> none  [device_terms(): lax.scan(tile_step, start_totals, tile_range)]
  transfers between devices with their start and end apart: 6 -> 0, of which waited for: 6 -> 0; matrix products, arithmetic and copies ran while one was open for 3% -> 0% of each run, Pallas kernels for 0% -> 0%
where the time goes in v3:
time: 91.7 us; the launch traced here: 91.2 us
  Pallas kernels  80.5 us (88%)
  local copies, waits for them, and re-layouts  10 us (11%)
    pallas_call x1, Pallas kernels, on_device(): pl.pallas_call(functools.partial(step_kernel, scale), in_specs=[vmem] * 7...  80.5 us
    unnamed x25, local copies, waits for them, and re-layouts  10 us

profile of v3, /device:TPU:1, one launch (start us, length us, event | category | flops | bytes accessed | tf_op | source)
XLA Modules:
  0.0 91.2 jit_solution(11350670125367447624)
XLA Ops:
  0.6 0.0 copy-start.8
  0.6 0.0 copy-start.9
  0.7 0.0 copy-start.10
  0.7 0.7 copy-done.8
  1.3 0.0 copy-done.9
  1.3 0.0 copy-done.10
  1.3 0.0 copy-start
  1.3 1.2 %copy-done = bf16[1,1024,512]{2,1,0:T(8,128)(2,1)S(1)} copy-done((bf16[1,1024,512]{2,1,0:T(8,128)(2,1)S(1)}, bf16[1,1024,512]{2,1,0:T(8,128)(2,1)}, u32[]{:S(2)}) %copy-start) | copy-done | bytes 1048600
  2.6 0.0 copy-start.1
  2.6 0.9 %copy-done.1 = bf16[1024,128]{1,0:T(8,128)(2,1)S(1)} copy-done((bf16[1024,128]{1,0:T(8,128)(2,1)S(1)}, bf16[1024,128]{1,0:T(8,128)(2,1)}, u32[]{:S(2)}) %copy-start.1) | copy-done | bytes 262168
  3.5 0.0 copy-start.2
  3.5 0.9 %copy-done.2 = bf16[4,256,128]{2,1,0:T(8,128)(2,1)S(1)} copy-done((bf16[4,256,128]{2,1,0:T(8,128)(2,1)S(1)}, bf16[4,256,128]{2,1,0:T(8,128)(2,1)}, u32[]{:S(2)}) %copy-start.2) | copy-done | bytes 262168
  4.5 0.0 copy-start.3
  4.5 0.9 %copy-done.3 = bf16[4,128,256]{2,1,0:T(8,128)(2,1)S(1)} copy-done((bf16[4,128,256]{2,1,0:T(8,128)(2,1)S(1)}, bf16[4,128,256]{2,1,0:T(8,128)(2,1)}, u32[]{:S(2)}) %copy-start.3) | copy-done | bytes 262168
  5.4 0.0 copy-start.4
  5.4 0.9 copy-done.4
  6.3 0.0 copy-start.5
  6.3 0.9 copy-done.5
  7.2 0.8 copy-done.6
  8.0 0.7 copy-done.7
  8.7 80.5 %step.1 = (f32[256,128]{1,0:T(8,128)S(1)}, f32[9,1,1024]{2,1,0:T(1,128)S(1)}, f32[128,512]{1,0:T(8,128)S(1)}) custom-call(s32[4,8]{1,0:T(4,128)S(1)} %bitcast.11, s32[1,4]{1,0:T(1,128)S(1)} %copy-done.10, s32[1,1024]{1,0:T(1,128)S(1)} %bitcast.10, bf16[1024,128]{1,0:T(8,128)(2,1)S(1)} %copy-done.1, f32[9,1,1024]{2,1,0:T(1,128)S(1)} %bitcast.8, ...), custom_call_target="tpu_custom_call" | custom-call | tf_op jit(solution)/shard_map/step/pallas_call | solution.py:523
  89.2 0.7 copy.17
  89.9 0.6 copy.18
  90.5 0.7 copy.19
  (2 shorter events, 0.0 us)
Async XLA Ops:
  0.6 0.7 copy-start.8
  0.6 0.7 copy-start.9
  0.7 0.7 copy-start.10
  1.3 1.2 %copy-start = (bf16[1,1024,512]{2,1,0:T(8,128)(2,1)S(1)}, bf16[1,1024,512]{2,1,0:T(8,128)(2,1)}, u32[]{:S(2)}) copy-start(bf16[1,1024,512]{2,1,0:T(8,128)(2,1)} %param.14) | copy-start | bytes 3145732
  2.6 0.9 %copy-start.1 = (bf16[1024,128]{1,0:T(8,128)(2,1)S(1)}, bf16[1024,128]{1,0:T(8,128)(2,1)}, u32[]{:S(2)}) copy-start(bf16[1024,128]{1,0:T(8,128)(2,1)} %feat_ref.1) | copy-start | bytes 786436
  3.5 0.9 %copy-start.2 = (bf16[4,256,128]{2,1,0:T(8,128)(2,1)S(1)}, bf16[4,256,128]{2,1,0:T(8,128)(2,1)}, u32[]{:S(2)}) copy-start(bf16[4,256,128]{2,1,0:T(8,128)(2,1)} %constant.7.clone.moments_hbm) | copy-start | bytes 786436
  4.5 0.9 %copy-start.3 = (bf16[4,128,256]{2,1,0:T(8,128)(2,1)S(1)}, bf16[4,128,256]{2,1,0:T(8,128)(2,1)}, u32[]{:S(2)}) copy-start(bf16[4,128,256]{2,1,0:T(8,128)(2,1)} %constant.6.clone.basis_hbm) | copy-start | bytes 786436
  5.4 0.9 copy-start.4
  6.3 0.9 copy-start.5
  7.2 0.8 copy-start.6
  8.0 0.7 copy-start.7

commit v4 on v3

--- a/solution.py
+++ b/solution.py
@@ -107,35 +107,26 @@
 
 
 class Exchange:
-    def __init__(self, pairs, sems):
-        self.pairs = pairs
-        self.sems = sems
-
-    def copies(self, stage, i):
+    def __init__(self, send, hop_a, hop_b, recv, sems):
+        self.send, self.hop_a, self.hop_b, self.recv, self.sems = send, hop_a, hop_b, recv, sems
+
+    def copy(self, stage, i):
         y, z, c, _ = place()
-        out = []
-        for n, (send, hop_a, hop_b, recv) in enumerate(self.pairs):
-            sems = self.sems.at[4 * n + stage]
-            if stage == 0:
-                to = (y + i) % Y
-                out.append(remote(send.at[to, :, c], hop_a.at[y], sems, i, {"gs": gs_of(to, z, c)}))
-            elif stage == 1:
-                to = (z + i) % Z
-                out.append(remote(send.at[:, to, 1 - c], hop_b.at[z], sems, i, {"gs": gs_of(y, to, 1 - c)}))
-            elif stage == 2:
-                to = (z + i) % Z
-                out.append(remote(hop_a.at[:, to], recv.at[:, z, c], sems, i, {"gs": gs_of(y, to, c)}))
-            else:
-                to = (y + i) % Y
-                out.append(remote(hop_b.at[:, to], recv.at[y, :, 1 - c], sems, i, {"gs": gs_of(to, z, c)}))
-        return out
+        sems = self.sems.at[stage]
+        if stage == 0:
+            to = (y + i) % Y
+            return remote(self.send.at[to, :, c], self.hop_a.at[y], sems, i, {"gs": gs_of(to, z, c)})
+        if stage == 1:
+            to = (z + i) % Z
+            return remote(self.send.at[:, to, 1 - c], self.hop_b.at[z], sems, i, {"gs": gs_of(y, to, 1 - c)})
+        if stage == 2:
+            to = (z + i) % Z
+            return remote(self.hop_a.at[:, to], self.recv.at[:, z, c], sems, i, {"gs": gs_of(y, to, c)})
+        to = (y + i) % Y
+        return remote(self.hop_b.at[:, to], self.recv.at[y, :, 1 - c], sems, i, {"gs": gs_of(to, z, c)})
 
     def each(self, stage, act):
-        def body(i):
-            for copy in self.copies(stage, i):
-                act(copy)
-
-        loop(0 if stage == 1 else 1, 8, body)
+        loop(0 if stage == 1 else 1, 8, lambda i: act(self.copy(stage, i)))
 
     def start(self, stage):
         self.each(stage, lambda copy: copy.start())
@@ -149,33 +140,35 @@
 
     def keep_first(self):
         y, z, c, _ = place()
-        for send, hop_a, hop_b, recv in self.pairs:
-            hop_a[y] = send[y, :, c]
+        self.hop_a[y] = self.send[y, :, c]
 
     def keep_a(self):
         y, z, c, _ = place()
-        for send, hop_a, hop_b, recv in self.pairs:
-            recv[:, z, c] = hop_a[:, z]
+        self.recv[:, z, c] = self.hop_a[:, z]
 
     def keep_b(self):
         y, z, c, _ = place()
-        for send, hop_a, hop_b, recv in self.pairs:
-            recv[y, :, 1 - c] = hop_b[:, y]
+        self.recv[y, :, 1 - c] = self.hop_b[:, y]
 
 
 def step_kernel(
-    scale, lists_ref, lengths_ref, order_ref, feat_ref, geo_in_ref, decoder_ref, images_ref,
-    teacher_hbm, basis_hbm, moments_hbm, tables_hbm,
-    feat_out, geo_out, dec_out,
-    teacher_ref, basis_ref, moments_ref, tables_ref, load_sems,
-    onehot, select, mask, source, gathered,
-    fsend_f, fsend_g, fa_f, fa_g, fb_f, fb_g, frecv_f, frecv_g, forward_sems,
-    geo_rows, geo, geo_grad, rows, columns, feat_t, alphas, weights, weights_b, inners, values, bias, totals, carry,
-    terms, right, acc, dec,
-    rsend_f, rsend_g, ra_f, ra_g, rb_f, rb_g, rrecv_f, rrecv_g, return_sems,
-    dec_tiles, d1, p1, d2, p2, d3, p3, d4, d5, sum_sems,
-    returned, shares, view_in, view_sems,
+    scale, *refs,
 ):
+    inputs, (feat_out, geo_out, dec_out), held, rest = refs[:11], refs[11:14], refs[14:25], refs[25:]
+    (
+        order_ref, feat_ref, geo_in_ref, decoder_ref, images_ref, lists_ref, lengths_ref,
+        teacher_ref, basis_ref, moments_ref, tables_ref,
+    ) = held
+    (
+        load_sems,
+        onehot, select, mask, source, gathered,
+        fsend_f, fsend_g, fa_f, fa_g, fb_f, fb_g, frecv_f, frecv_g, forward_sems_f, forward_sems_g,
+        geo_rows, geo, geo_grad, rows, columns, feat_t, alphas, weights, weights_b, gparts, inners, values, bias, totals, carry,
+        laters, terms, left, right, acc, dec,
+        rsend_f, rsend_g, ra_f, ra_g, rb_f, rb_g, rrecv_f, rrecv_g, return_sems_f, return_sems_g,
+        dec_tiles, d1, p1, d2, p2, d3, p3, d4, d5, sum_sems,
+        returned, shares, view_in, view_sems,
+    ) = rest
     y, z, c, x = place()
     count = feat_ref.shape[0]
     tiles = lists_ref.shape[0]
@@ -183,10 +176,7 @@
     corner = x * C + c
 
     loads = [
-        pltpu.make_async_copy(src, dst, load_sems.at[n])
-        for n, (src, dst) in enumerate((
-            (teacher_hbm, teacher_ref), (basis_hbm, basis_ref), (moments_hbm, moments_ref), (tables_hbm, tables_ref)
-        ))
+        pltpu.make_async_copy(src, dst, load_sems.at[n]) for n, (src, dst) in enumerate(zip(inputs, held))
     ]
     for load in loads:
         load.start()
@@ -203,47 +193,57 @@
     greet(1, X, lambda i: {"gs": gs_of(y, z, c), "view": (x + i) % X})
     greet(1, X, lambda i: {"gs": gs_of(y, z, 1 - c), "view": (x + i) % X})
 
+    for load in loads[:3]:
+        load.wait()
     row = lax.broadcasted_iota(jnp.int32, (128, count), 0)
     column = lax.broadcasted_iota(jnp.int32, (128, count), 1)
     select[...] = jnp.where(row == jnp.right_shift(column, 3), 1.0, 0.0).astype(BF16)
     mask[...] = jnp.where(jnp.right_shift(row, 4) == jnp.bitwise_and(column, 7), 1.0, 0.0)
-    for n in range(nblocks):
-        span = slice(n * BLK, (n + 1) * BLK)
-        source[0:FEAT, span] = feat_ref[span, :].astype(F32).T.astype(BF16)
     padded = jnp.concatenate([geo_in_ref[n] for n in range(9)] + [jnp.zeros((7, count), F32)], 0)
-    for index, part in enumerate(pieces(padded, 3)):
-        source[FEAT + 16 * index : FEAT + 16 * index + 16, :] = part
+    source[...] = jnp.concatenate([part.astype(F32) for part in pieces(padded, 3)], 0).astype(BF16)
     step = 2 * Z * C * SEND
     for n in range(count // step):
         span = slice(n * step, (n + 1) * step)
         row = lax.broadcasted_iota(jnp.int32, (count, step), 0)
         hot = jnp.where(row == order_ref[:, span], 1.0, 0.0).astype(BF16)
         onehot[:, span] = hot
-        picked = dot(source[...], hot)
-        fsend_f[n * 2 : n * 2 + 2] = picked[0:FEAT, :].T.reshape(2, Z, C, SEND, FEAT).astype(BF16)
-        gathered[:, span] = picked[FEAT : FEAT + 48, :]
+        gathered[:, span] = dot(source[...], hot)
     sent_rows = to_rows([gathered[16 * i : 16 * i + 16, :] for i in range(3)], select[...], mask[...])
     for d in range(Y * Z * C):
         fsend_g[d // (Z * C), (d // C) % Z, d % C] = sent_rows[d : d + 1, :]
 
     pl.semaphore_wait(barrier, Y - 1 + Z - 1 + Z + 2 * (X - 1))
-    forward = Exchange([(fsend_f, fa_f, fb_f, frecv_f), (fsend_g, fa_g, fb_g, frecv_g)], forward_sems)
-    forward.start(0)
-    forward.start(1)
-    forward.keep_first()
+    forward_g = Exchange(fsend_g, fa_g, fb_g, frecv_g, forward_sems_g)
+    forward_f = Exchange(fsend_f, fa_f, fb_f, frecv_f, forward_sems_f)
+    forward_g.start(0)
+    forward_g.start(1)
+    forward_g.keep_first()
+    turned = feat_ref[...].astype(F32).T.astype(BF16)
+    for n in range(count // step):
+        picked = dot(turned, onehot[:, n * step : (n + 1) * step])
+        fsend_f[n * 2 : n * 2 + 2] = picked.T.reshape(2, Z, C, SEND, FEAT).astype(BF16)
+    forward_f.start(0)
+    forward_f.start(1)
+    forward_f.keep_first()
+    forward_g.arrive(0)
+    forward_g.start(2)
+    forward_g.keep_a()
+    forward_g.arrive(1)
+    forward_g.start(3)
+    forward_g.keep_b()
     acc[...] = jnp.zeros_like(acc)
     dec[...] = jnp.zeros_like(dec)
     rows[...] = jnp.zeros_like(rows)
-    forward.arrive(0)
-    forward.start(2)
-    forward.keep_a()
-    forward.arrive(1)
-    forward.start(3)
-    forward.keep_b()
-    for load in loads:
+    forward_f.arrive(0)
+    forward_f.start(2)
+    forward_f.keep_a()
+    forward_f.arrive(1)
+    forward_f.start(3)
+    forward_f.keep_b()
+    for load in loads[3:]:
         load.wait()
-    forward.arrive(2)
-    forward.arrive(3)
+    forward_g.arrive(2)
+    forward_g.arrive(3)
 
     for d in range(Y * Z * C):
         geo_rows[d : d + 1, :] = frecv_g[d // (Z * C), (d // C) % Z, d % C]
@@ -280,11 +280,8 @@
         rows[3 * index : 3 * index + 3, :] = part.astype(F32)
     for n in range(nblocks):
         span = slice(n * BLK, (n + 1) * BLK)
-        block = frecv_f[n].astype(F32).reshape(BLK, FEAT)
-        columns[span, 0:FEAT] = block.astype(BF16)
         columns[span, FEAT : 2 * FEAT] = rows[:, span].T.astype(BF16)
-        feat_t[0:FEAT, span] = block.T.astype(BF16)
-        feat_t[FEAT : FEAT + 32, span] = rows[0:32, span].astype(BF16)
+    feat_t[FEAT : FEAT + 32, :] = rows[0:32, :].astype(BF16)
 
     def xc(i):
         to = (corner + i) % (X * C)
@@ -313,7 +310,25 @@
     def sum_arrive(stage):
         loop(1, 8, lambda i: sum_copy(stage, i).wait_recv())
 
-    def tile_step(tile):
+    def sum_step(stage):
+        sum_arrive(stage)
+        if stage == 0:
+            p1[...] = sum(d1[i] for i in range(X * C))
+            sum_start(1)
+            d2[z] = p1[z]
+        elif stage == 1:
+            p2[...] = sum(d2[i] for i in range(Z))
+            sum_start(2)
+            d3[y] = p2[...]
+        elif stage == 2:
+            p3[...] = sum(d3[i] for i in range(Y)) * scale
+            sum_start(3)
+            d4[z] = p3[...]
+        else:
+            sum_start(4)
+            d5[corner] = d4[...]
+
+    def weigh(tile):
         block_i = lax.broadcasted_iota(jnp.int32, (LIST, LIST), 0)
         slot_i = lax.broadcasted_iota(jnp.int32, (LIST, LIST), 1)
         slot_col = jnp.sum(
@@ -321,7 +336,7 @@
         )
         slot_row = jnp.sum(jnp.where(block_i == slot_i, slot_col, 0.0), axis=0, keepdims=True)
         earlier = jnp.where(slot_row < slot_col, 1.0, 0.0)
-        later = jnp.where(slot_row > slot_col, 1.0, 0.0)
+        laters[tile] = jnp.where(slot_row > slot_col, 1.0, 0.0)
         tile_i = lax.broadcasted_iota(jnp.int32, lengths_ref.shape, 1)
         length = jnp.sum(jnp.where(tile_i == tile, lengths_ref[...].astype(F32), 0.0), axis=1, keepdims=True)
         bias[...] = jnp.broadcast_to(jnp.where(slot_col < length, 0.0, -1e30), (LIST, PIX))
@@ -336,18 +351,19 @@
             high, low = pieces(log_keep, 2)
             inner = dot(tables_ref[0], jnp.concatenate([high, low], 0))
             totals[n : n + 1, :] = inner[BLK - 1 : BLK, :] + log_keep[BLK - 1 : BLK, :]
-            alphas[span, :] = alpha
+            alphas[tile, span, :] = alpha
             inners[span, :] = inner
         carry[...] = sum(earlier[:, n : n + 1] * totals[n : n + 1, :] for n in range(LIST))
         for n in range(LIST):
             span = slice(n * BLK, (n + 1) * BLK)
-            weight = alphas[span, :] * jnp.exp2(inners[span, :] + carry[n : n + 1, :])
+            weight = alphas[tile, span, :] * jnp.exp2(inners[span, :] + carry[n : n + 1, :])
             weight_b, weight_low = pieces(weight, 2)
-            weights[span, :] = weight
-            weights_b[span, 0:PIX] = weight_b
-            weights_b[span, PIX : 2 * PIX] = weight_low
-        total = dot(feat_t[...], weights_b[:, 0:PIX])
-        total_low = dot(feat_t[FEAT:, :], weights_b[:, PIX : 2 * PIX])
+            weights[tile, span, :] = weight
+            weights_b[tile, span, 0:PIX] = weight_b
+            weights_b[tile, span, PIX : 2 * PIX] = weight_low
+    def render(tile):
+        total = dot(feat_t[...], weights_b[tile, :, 0:PIX])
+        total_low = dot(feat_t[FEAT:, :], weights_b[tile, :, PIX : 2 * PIX])
 
         rendered_t = total[0:FEAT, :].astype(BF16)
         color = (
@@ -362,56 +378,72 @@
         gpred = (error * lax.rsqrt(error * error + 0.04)).astype(BF16)
         dec[...] += dot(rendered_t, gpred)
 
-        @pl.when(tile == tiles - 1)
-        def _():
-            for n in range(FEAT * CT // 1024):
-                row, lane = n // (CT // 128), n % (CT // 128)
-                dec_tiles[n // Z, n % Z] = dec[8 * row : 8 * row + 8, 128 * lane : 128 * lane + 128]
-            sum_start(0)
-
         terms[0:FEAT, :] = dot_t(decoder_ref[...], gpred)
         terms[FEAT:, :] = jnp.zeros_like(terms[FEAT:, :])
         for index, part in enumerate([pieces(gcolor, 3)[n] for n in (0, 1, 0, 2, 1, 0)]):
             terms[FEAT + 3 * index : FEAT + 3 * index + 3, :] = part.astype(F32)
-        right[...] = terms[...].T.astype(BF16)
-
-        values[...] = dot(columns[...], terms[...].astype(BF16))
+        left[tile] = terms[...].astype(BF16)
+        right[tile] = terms[...].T.astype(BF16)
+
+    def differentiate(tile):
+        values[...] = dot(columns[...], left[tile])
         for n in range(LIST):
             span = slice(n * BLK, (n + 1) * BLK)
-            value = values[span, :] * weights[span, :]
+            value = values[span, :] * weights[tile, span, :]
             high, low = pieces(value, 2)
             inner = dot(tables_ref[1], jnp.concatenate([high, low], 0))
             totals[n : n + 1, :] = inner[0:1, :] + value[0:1, :]
             values[span, :] = value
             inners[span, :] = inner
+        later = laters[tile]
         carry[...] = sum(later[:, n : n + 1] * totals[n : n + 1, :] for n in range(LIST))
         for n in range(LIST):
             span = slice(n * BLK, (n + 1) * BLK)
-            alpha = alphas[span, :]
+            alpha = alphas[tile, span, :]
             square = alpha * alpha
             ratio = alpha + square
             ratio = ratio + ratio * square
             ratio = ratio + ratio * (square * square)
             gexponent = values[span, :] - ratio * (inners[span, :] + carry[n : n + 1, :])
             high, low = pieces(gexponent, 2)
-            weights_b[span, 2 * PIX : 3 * PIX] = high
-            weights_b[span, 3 * PIX : 4 * PIX] = low
+            gparts[span, 0:PIX] = high
+            gparts[span, PIX : 2 * PIX] = low
         moments = moments_ref[tile]
-        acc[...] += dot(weights_b[:, 0:PIX], right[...])
-        acc[:, FEAT:] += dot(weights_b[:, PIX:], jnp.concatenate([right[:, FEAT:], moments, moments], 0))
-
-    loop(0, tiles, tile_step)
-
-    backward = Exchange([(rsend_f, ra_f, rb_f, rrecv_f), (rsend_g, ra_g, rb_g, rrecv_g)], return_sems)
-    d1[corner] = dec_tiles[corner]
-    sum_arrive(0)
-    p1[...] = sum(d1[i] for i in range(X * C))
-    sum_start(1)
-    d2[z] = p1[z]
-
+        acc[...] += dot(weights_b[tile, :, 0:PIX], right[tile])
+        acc[:, FEAT:] += dot(weights_b[tile, :, PIX:], right[tile, :, FEAT:]) + dot(
+            gparts[...], jnp.concatenate([moments, moments], 0)
+        )
+        for stage in range(3):
+
+            @pl.when(tile == stage + 1)
+            def _():
+                sum_step(stage)
+
+    loop(0, tiles, weigh)
+    forward_f.arrive(2)
+    forward_f.arrive(3)
     for n in range(nblocks):
         span = slice(n * BLK, (n + 1) * BLK)
-        rsend_f[n] = acc[span, 0:FEAT].reshape(Z, C, SEND, FEAT)
+        block = frecv_f[n].astype(F32).reshape(BLK, FEAT)
+        columns[span, 0:FEAT] = block.astype(BF16)
+        feat_t[0:FEAT, span] = block.T.astype(BF16)
+    loop(0, tiles, render)
+    for n in range(FEAT * CT // 1024):
+        row, lane = n // (CT // 128), n % (CT // 128)
+        dec_tiles[n // Z, n % Z] = dec[8 * row : 8 * row + 8, 128 * lane : 128 * lane + 128]
+    sum_start(0)
+    d1[corner] = dec_tiles[corner]
+    loop(0, tiles, differentiate)
+
+    backward_f = Exchange(rsend_f, ra_f, rb_f, rrecv_f, return_sems_f)
+    backward_g = Exchange(rsend_g, ra_g, rb_g, rrecv_g, return_sems_g)
+    for n in range(nblocks):
+        rsend_f[n] = acc[n * BLK : (n + 1) * BLK, 0:FEAT].reshape(Z, C, SEND, FEAT)
+    backward_f.start(0)
+    backward_f.start(1)
+    backward_f.keep_first()
+    for n in range(nblocks):
+        span = slice(n * BLK, (n + 1) * BLK)
         rows[:, span] = acc[span, FEAT:].T
     gx, gy, ca, cc, slope, reach = parameters()
     cb = slope * reach
@@ -434,33 +466,29 @@
     for d in range(Y * Z * C):
         rsend_g[d // (Z * C), (d // C) % Z, d % C] = back_rows[d : d + 1, :]
 
-    backward.start(0)
-    backward.start(1)
-    backward.keep_first()
-    sum_arrive(1)
-    p2[...] = sum(d2[i] for i in range(Z))
-    sum_start(2)
-    d3[y] = p2[...]
-    backward.arrive(0)
-    backward.start(2)
-    backward.keep_a()
-    backward.arrive(1)
-    backward.start(3)
-    backward.keep_b()
-    sum_arrive(2)
-    p3[...] = sum(d3[i] for i in range(Y)) * scale
-    sum_start(3)
-    d4[z] = p3[...]
-    sum_arrive(3)
-    sum_start(4)
-    d5[corner] = d4[...]
-    backward.arrive(2)
-    backward.arrive(3)
-
-    for d in range(Y * Z * C):
-        geo_rows[d : d + 1, :] = rrecv_g[d // (Z * C), (d // C) % Z, d % C]
-    geo_back = from_rows(geo_rows[...], select[...], mask[...])
-    geo_parts = jnp.concatenate([part.astype(F32) for part in pieces(geo_back, 3)], 0).astype(BF16)
+    backward_g.start(0)
+    backward_g.start(1)
+    backward_g.keep_first()
+    sum_step(3)
+    backward_f.arrive(0)
+    backward_f.start(2)
+    backward_f.keep_a()
+    backward_f.arrive(1)
+    backward_f.start(3)
+    backward_f.keep_b()
+    backward_g.arrive(0)
+    backward_g.start(2)
+    backward_g.keep_a()
+    backward_g.arrive(1)
+    backward_g.start(3)
+    backward_g.keep_b()
+    sum_arrive(4)
+    for n in range(FEAT * CT // 1024):
+        row, lane = n // (CT // 128), n % (CT // 128)
+        dec_out[8 * row : 8 * row + 8, 128 * lane : 128 * lane + 128] = d5[n // Z, n % Z]
+    backward_f.arrive(2)
+    backward_f.arrive(3)
+
     for n in range(Y):
         high, low = pieces(rrecv_f[n].reshape(Z * C * SEND, FEAT), 2)
         span = slice(n * Z * C * SEND, (n + 1) * Z * C * SEND)
@@ -480,14 +508,16 @@
             view_copy(i).start()
         else:
             view_in[x] = share
+    backward_g.arrive(2)
+    backward_g.arrive(3)
+    for d in range(Y * Z * C):
+        geo_rows[d : d + 1, :] = rrecv_g[d // (Z * C), (d // C) % Z, d % C]
+    geo_back = from_rows(geo_rows[...], select[...], mask[...])
+    geo_parts = jnp.concatenate([part.astype(F32) for part in pieces(geo_back, 3)], 0).astype(BF16)
     own = dot_t(geo_parts, onehot[...])
     own = own[0:16] + own[16:32] + own[32:48]
     for n in range(9):
         geo_out[n] = own[n : n + 1]
-    sum_arrive(4)
-    for n in range(FEAT * CT // 1024):
-        row, lane = n // (CT // 128), n % (CT // 128)
-        dec_out[8 * row : 8 * row + 8, 128 * lane : 128 * lane + 128] = d5[n // Z, n % Z]
     for i in (1, 2, 3):
         view_copy(i).wait_recv()
     feat_out[...] = view_in[0] + view_in[1] + view_in[2] + view_in[3]
@@ -495,8 +525,8 @@
         view_copy(i).wait_send()
     for stage in range(5):
         loop(1, 8, lambda i: sum_copy(stage, i).wait_send())
-    forward.sent()
-    backward.sent()
+    for exchange in (forward_f, forward_g, backward_f, backward_g):
+        exchange.sent()
 
 
 def exchange_buffers(dtype):
@@ -506,7 +536,7 @@
         pltpu.VMEM((Y, Z, SEND, FEAT), dtype), pltpu.VMEM((Y, Z, 1, 128), geo_dtype),
         pltpu.VMEM((Z, Y, SEND, FEAT), dtype), pltpu.VMEM((Z, Y, 1, 128), geo_dtype),
         pltpu.VMEM((*GROUP, SEND, FEAT), dtype), pltpu.VMEM((*GROUP, 1, 128), geo_dtype),
-        pltpu.SemaphoreType.DMA((8, 2, 8)),
+        pltpu.SemaphoreType.DMA((4, 2, 8)), pltpu.SemaphoreType.DMA((4, 2, 8)),
     ]
 
 
@@ -520,9 +550,13 @@
     vmem = pl.BlockSpec(memory_space=pltpu.VMEM)
     hbm = pl.BlockSpec(memory_space=pl.ANY)
     tile = (8, 128)
+    inputs = (
+        send_index[0], features, geometry.reshape(9, 1, count), decoder, images.reshape(3, 1, tiles * PIX),
+        tile_lists[0], tile_lengths, teacher[0], jnp.asarray(basis), jnp.asarray(moments), jnp.asarray(tables),
+    )
     feature_grad, geo_own, decoder_grad = pl.pallas_call(
         functools.partial(step_kernel, scale),
-        in_specs=[vmem] * 7 + [hbm] * 4,
+        in_specs=[hbm] * len(inputs),
         out_specs=[vmem] * 3,
         out_shape=[
             jax.ShapeDtypeStruct((quarter, FEAT), F32),
@@ -530,15 +564,12 @@
             jax.ShapeDtypeStruct((FEAT, CT), F32),
         ],
         scratch_shapes=[
-            pltpu.VMEM((tiles * PIX, CT), BF16),
-            pltpu.VMEM(basis.shape, BF16),
-            pltpu.VMEM(moments.shape, BF16),
-            pltpu.VMEM(tables.shape, BF16),
-            pltpu.SemaphoreType.DMA((4,)),
+            *(pltpu.VMEM(array.shape, array.dtype) for array in inputs),
+            pltpu.SemaphoreType.DMA((len(inputs),)),
             pltpu.VMEM((count, count), BF16),
             pltpu.VMEM((128, count), BF16),
             pltpu.VMEM((128, count), F32),
-            pltpu.VMEM((FEAT + 48, count), BF16),
+            pltpu.VMEM((48, count), BF16),
             pltpu.VMEM((48, count), F32),
             *exchange_buffers(BF16),
             pltpu.VMEM((128, 128), F32),
@@ -547,16 +578,19 @@
             pltpu.VMEM((128, count), F32),
             pltpu.VMEM((count, 2 * FEAT), BF16),
             pltpu.VMEM((FEAT + 32, count), BF16),
-            pltpu.VMEM((LIST * BLK, PIX), F32),
-            pltpu.VMEM((LIST * BLK, PIX), F32),
-            pltpu.VMEM((LIST * BLK, 4 * PIX), BF16),
-            pltpu.VMEM((LIST * BLK, PIX), F32),
-            pltpu.VMEM((LIST * BLK, PIX), F32),
+            pltpu.VMEM((tiles, count, PIX), F32),
+            pltpu.VMEM((tiles, count, PIX), F32),
+            pltpu.VMEM((tiles, count, 2 * PIX), BF16),
+            pltpu.VMEM((count, 2 * PIX), BF16),
+            pltpu.VMEM((count, PIX), F32),
+            pltpu.VMEM((count, PIX), F32),
             pltpu.VMEM((LIST, PIX), F32),
             pltpu.VMEM((LIST, PIX), F32),
             pltpu.VMEM((LIST, PIX), F32),
+            pltpu.VMEM((tiles, LIST, LIST), F32),
             pltpu.VMEM((2 * FEAT, PIX), F32),
-            pltpu.VMEM((PIX, 2 * FEAT), BF16),
+            pltpu.VMEM((tiles, 2 * FEAT, PIX), BF16),
+            pltpu.VMEM((tiles, PIX, 2 * FEAT), BF16),
             pltpu.VMEM((count, 2 * FEAT), F32),
             pltpu.VMEM((FEAT, CT), F32),
             *exchange_buffers(F32),
@@ -575,15 +609,9 @@
             pltpu.VMEM((X, quarter, FEAT), F32),
             pltpu.SemaphoreType.DMA((2, X)),
         ],
-        compiler_params=pltpu.CompilerParams(
-            collective_id=0, has_side_effects=True, vmem_limit_bytes=48 * 1024 * 1024
-        ),
+        compiler_params=pltpu.CompilerParams(collective_id=0, has_side_effects=True),
         name="step",
-    )(
-        tile_lists[0], tile_lengths, send_index[0], features, geometry.reshape(9, 1, count), decoder,
-        images.reshape(3, 1, tiles * PIX), teacher[0],
-        jnp.asarray(basis), jnp.asarray(moments), jnp.asarray(tables),
-    )
+    )(*inputs)
     return (feature_grad, geo_own.reshape(1, 9, count), decoder_grad)
 
 

time: 91.7 us -> 79.8 us (0.87)
  the two profiles are of different devices: /device:TPU:1 before, /device:TPU:2 now
where the time goes in v4:
time: 79.8 us; the launch traced here: 79.6 us
  Pallas kernels  75.2 us (94%)
  local copies, waits for them, and re-layouts  3.7 us (5%)
    pallas_call x1, Pallas kernels, on_device(): pl.pallas_call(functools.partial(step_kernel, scale), in_specs=[hbm] * le...  75.2 us
    unnamed x5, local copies, waits for them, and re-layouts  3.7 us

profile of v4, /device:TPU:2, one launch (start us, length us, event | category | flops | bytes accessed | tf_op | source)
XLA Modules:
  0.0 79.6 jit_solution(278390635502704259)
XLA Ops:
  0.6 75.2 %step.1 = (f32[256,128]{1,0:T(8,128)}, f32[9,1,1024]{2,1,0:T(1,128)}, f32[128,512]{1,0:T(8,128)}) custom-call(s32[1,1024]{1,0:T(1,128)} %bitcast.10, bf16[1024,128]{1,0:T(8,128)(2,1)} %refs_1_.1, f32[9,1,1024]{2,1,0:T(1,128)} %bitcast.8, bf16[128,512]{1,0:T(8,128)(2,1)} %refs_3_.1, f32[3,1,1024]{2,1,0:T(1,128)} %bitcast.9, s32[4,8]{1,0:T(4,128)} %bitcast.11, ...), custom_call_target="tpu_custom_call" | custom-call | tf_op jit(solution)/shard_map/step/pallas_call | solution.py:557
  75.9 0.0 copy-start
  75.9 1.6 %copy.17 = f32[256,128]{1,0:T(8,128)} copy(f32[256,128]{1,0:T(8,128)} %get-tuple-element.12) | data formatting | bytes 262144
  77.5 1.4 %copy.18 = f32[1,9,1024]{2,0,1:T(1,128)} copy(f32[1,9,1024]{2,0,1:T(1,128)} %bitcast.7) | data formatting | bytes 73728
  78.9 0.0 copy-done
  78.9 0.7 copy.19
Async XLA Ops:
  75.9 3.0 %copy-start = (f32[128,512]{1,0:T(8,128)S(1)}, f32[128,512]{1,0:T(8,128)}, u32[]{:S(2)}) copy-start(f32[128,512]{1,0:T(8,128)} %get-tuple-element.14) | copy-start | bytes 786436
